TPU v7x, 512 devices: a whole 4x4x16 slice. The times are simulated.
512 devices in a mesh: gx: 16 (over z), gy: 32 (over y, x, core).
Axes of the slice: x: 4, y: 4, z: 16, core: 2. Of those that a mesh axis runs over, the one named last changes fastest.
Arguments:
- positions: float32 [2, 8388608], P(None, ('gx', 'gy')), may hold values from 0 to 4
- displacement: float32 [2, 8388608], P(None, ('gx', 'gy')), may hold values from -6 to 6
- velocity: float32 [2, 8388608], P(None, ('gx', 'gy')), may hold values from -6 to 6
- stiffness: float32 [8388608], P(('gx', 'gy')), may hold values from 0.5 to 4
- density: float32 [8388608], P(('gx', 'gy')), may hold values from 0.5 to 2
- move_rows: int32 [2097152], P(('gx', 'gy')), may hold values from 0 to 16383, as said below
- move_slot: int32 [2097152], P(('gx', 'gy')), may hold values from 0 to 8191, as said below
- move_new: int32 [2097152], P(('gx', 'gy')), may hold values from 0 to 16383, as said below
- edge_rows: int32 [4, 524288], P(None, ('gx', 'gy')), may hold values from 0 to 16383
- corner_rows: int32 [4, 32768], P(None, ('gx', 'gy')), may hold values from 0 to 16383
- tile_src: int32 [196608], P(('gx', 'gy')), may hold values from 0 to 161
- bond_bits: int32 [196608, 2048], P(('gx', 'gy')), may hold values from 0 to 255
Outputs:
- speeds_after_update: float32 [2, 8388608], P(None, ('gx', 'gy'))
- moved_offsets_after: float32 [2, 8388608], P(None, ('gx', 'gy'))
Inputs may be any that keep to these rules, and one draw needn't show every extreme that they name: `move_rows`: each owner's 4096 entries are distinct rows of its own points. `move_slot`: each owner's entries are distinct; no owner sends more than 256 points to one destination, and every owner sends exactly 256 to some destination. `move_new`: the rows at which an owner receives points are exactly its own move_rows, each once.
All inputs are finite; a program needn't handle non-finite values.
Results may differ from a plain program's by a relative error of at most 0.00002.
Values sent between devices are 32-bit elements; how exact they have to be, the bound alone decides.
No kernel may reach another device: no remote copies, remote signals or barrier semaphores. Data moves between devices by JAX's collectives and lax.ppermute only.
A program may use at most 128 MiB of HBM per device.

v0:
```python
import math

import jax
import jax.numpy as jnp
from jax import lax
from jax.sharding import PartitionSpec as P

BLOCK = 128
PER_BLOCK = 3


NEAR_FLOOR = 0.5
BOND_COEFFICIENT = 0.005
SHIFT_STEP_SIZE = 0.5


def passed_along(block, axis, distance):
    devices = range(lax.axis_size(axis))
    route = [(i - distance, i) for i in devices if i - distance in devices]
    return lax.ppermute(block, axis, route)


def unpack(bond_words):
    lead = bond_words.shape[:-1]
    rows_words = bond_words.reshape(lead + (BLOCK, BLOCK // 8))
    widened = jnp.repeat(rows_words, 8, axis=-1)
    shifts = jnp.arange(BLOCK, dtype=jnp.int32) % 8
    return jnp.bitwise_and(jnp.right_shift(widened, shifts), 1).astype(jnp.float32)


def tile_forces(target, source, bond_words):
    intact = unpack(bond_words)
    sep_x = source[0][:, None, :] - target[0][:, :, None]
    sep_y = source[1][:, None, :] - target[1][:, :, None]
    rel_x = source[2][:, None, :] - target[2][:, :, None]
    rel_y = source[3][:, None, :] - target[3][:, :, None]
    separation = jnp.sqrt(sep_x * sep_x + sep_y * sep_y)
    inverse = 1.0 / jnp.maximum(separation, NEAR_FLOOR)
    weight = (
        intact
        * (sep_x * rel_x + sep_y * rel_y)
        * inverse
        * inverse
        * inverse
        * source[4][:, None, :]
    )
    push_x = jnp.sum(weight * sep_x, axis=2) * target[4]
    push_y = jnp.sum(weight * sep_y, axis=2) * target[4]
    return jnp.stack([push_x, push_y])


def body(
    positions,
    displacement,
    velocity,
    stiffness,
    density,
    move_rows,
    move_slot,
    move_new,
    edge_rows,
    corner_rows,
    tile_src,
    bond_bits,
):
    ledger_item = jnp.concatenate(
        [positions, displacement, velocity, stiffness[None], density[None]], 0
    )
    own_count = ledger_item.shape[1]
    slot_span = 2 * move_rows.shape[0]
    target_position_index = (
        jnp.full((1, slot_span), own_count, jnp.int32).at[0, move_slot].set(move_new)
    )
    front_rows = jnp.concatenate([ledger_item[0:4], ledger_item[6:7]], 0)
    state_rows = jnp.concatenate([ledger_item[4:6], ledger_item[7:8]], 0)
    empty = jnp.zeros((ledger_item.shape[0], slot_span), jnp.float32)
    arrived = lax.all_to_all(
        empty.at[:, move_slot].set(ledger_item[:, move_rows]),
        "gy",
        split_axis=1,
        concat_axis=1,
        tiled=True,
    )
    placed = lax.all_to_all(target_position_index, "gy", split_axis=1, concat_axis=1, tiled=True)
    ledger_item = ledger_item.at[:, placed[0]].set(arrived, mode="drop")
    front_rows = jnp.concatenate([ledger_item[0:4], ledger_item[6:7]], 0)
    state_rows = jnp.concatenate([ledger_item[4:6], ledger_item[7:8]], 0)
    carried_message_content = jnp.concatenate([front_rows[0:4], jnp.sqrt(front_rows[4:5])], 0)
    halo_len = edge_rows.shape[1]
    corner_len = corner_rows.shape[1]
    edge_out = carried_message_content[:, edge_rows]
    corner_out = carried_message_content[:, corner_rows]
    across = {}
    for shift_by, edge_index, corner_first, corner_second in ((-1, 0, 0, 1), (1, 3, 2, 3)):
        bundle = jnp.concatenate(
            [edge_out[:, edge_index], corner_out[:, corner_first], corner_out[:, corner_second]], 1
        )
        across[shift_by] = passed_along(bundle, "gx", shift_by)
    beside = {}
    for shift_by, edge_index, corner_start in ((-1, 1, halo_len), (1, 2, halo_len + corner_len)):
        lower = across[-1][:, corner_start : corner_start + corner_len]
        upper = across[1][:, corner_start : corner_start + corner_len]
        bundle = jnp.concatenate([edge_out[:, edge_index], lower, upper], 1)
        beside[shift_by] = passed_along(bundle, "gy", shift_by)
    edges = [
        across[-1][:, :halo_len],
        beside[-1][:, :halo_len],
        beside[1][:, :halo_len],
        across[1][:, :halo_len],
    ]
    first_cut = halo_len + corner_len
    corners = [
        beside[-1][:, halo_len:first_cut],
        beside[1][:, halo_len:first_cut],
        beside[-1][:, first_cut:],
        beside[1][:, first_cut:],
    ]
    used_cols = own_count + 4 * halo_len + 4 * corner_len
    ext_cols = -(-used_cols // BLOCK) * BLOCK
    filler = jnp.zeros((5, ext_cols - used_cols), jnp.float32)
    extended = jnp.concatenate([carried_message_content] + edges + corners + [filler], 1).reshape(
        5, -1, BLOCK
    )
    own_blocks = own_count // BLOCK
    group_blocks = math.gcd(own_blocks, 8)
    groups = own_blocks // group_blocks
    group_width = group_blocks * PER_BLOCK
    word_groups = bond_bits.reshape(groups, group_width, -1)
    source_groups = tile_src.reshape(groups, group_width)

    def group_push(operands):
        group_index, source_ids, bond_words = operands
        owned_part = lax.dynamic_slice_in_dim(extended, group_index * group_blocks, group_blocks, 1)
        target = jnp.repeat(owned_part, PER_BLOCK, axis=1)
        pushes = tile_forces(target, extended[:, source_ids], bond_words)
        return pushes.reshape(2, group_blocks, PER_BLOCK, BLOCK).sum(2)

    group_sums = lax.map(
        group_push, (jnp.arange(groups, dtype=jnp.int32), source_groups, word_groups)
    )
    summed_pull = jnp.moveaxis(group_sums, 1, 0).reshape(2, own_count)
    speeds_after_update = state_rows[0:2] + BOND_COEFFICIENT * summed_pull / state_rows[2]
    moved_offsets_after = front_rows[2:4] + SHIFT_STEP_SIZE * speeds_after_update
    return (speeds_after_update, moved_offsets_after)


def solution(mesh):
    placed = (
        P(None, ("gx", "gy")),
        P(None, ("gx", "gy")),
        P(None, ("gx", "gy")),
        P(("gx", "gy")),
        P(("gx", "gy")),
        P(("gx", "gy")),
        P(("gx", "gy")),
        P(("gx", "gy")),
        P(None, ("gx", "gy")),
        P(None, ("gx", "gy")),
        P(("gx", "gy")),
        P(("gx", "gy"), None),
    )
    return jax.shard_map(
        body,
        mesh=mesh,
        in_specs=placed,
        out_specs=(P(None, ("gx", "gy")), P(None, ("gx", "gy"))),
        check_vma=False,
    )
```

profile of v0, /device:TPU:392, one launch (start us, length us, event | category | flops | bytes accessed | tf_op | source)
XLA Modules:
  0.0 351.4 jit_solution(2855686995061008726)
XLA Ops:
  3.0 16.3 %scatter_custom_fusion.2 = s32[8192]{0:T(1024)} fusion(s32[4096]{0:T(1024)S(1)} %broadcast_select_fusion, s32[4096]{0:T(1024)} %param.21, s32[]{:T(128)} %constant.85.clone.1), kind=kCustom, calls=%fused_computation.66 | custom fusion | bytes 33280
  19.2 7.5 %all-to-all-start = ((s32[1,32,256]{2,0,1:T(1,128)}), s32[1,32,256]{2,0,1:T(1,128)S(1)}, u32[]{:S(2)}, u32[]{:S(2)}) async-start(s32[1,32,256]{2,0,1:T(1,128)} %bitcast.18), calls=%async_computation | async-start | bytes 65536 | tf_op jit(solution)/shard_map/all_to_all | solution.py:84
  29.7 5.3 %copy.100 = f32[8,16384]{0,1:T(8,128)} copy(f32[8,16384]{1,0:T(8,128)S(1)} %concatenate.28) | data formatting | bytes 1048576 | tf_op jit(solution)/shard_map/concatenate | solution.py:66
  35.0 35.8 %scatter_custom_fusion = f32[8,8192]{0,1:T(8,128)} fusion(s32[4096]{0:T(1024)S(1)} %get-tuple-element.167, f32[8,16384]{0,1:T(8,128)} %copy.100, s32[4096]{0:T(1024)S(1)} %get-tuple-element.168, f32[]{:T(128)} %constant.88.clone.1), kind=kCustom, calls=%fused_computation.48 | custom fusion | bytes 262656 | tf_op jit(solution)/shard_map/scatter | solution.py:78
  70.8 3.4 copy.99
  74.2 7.5 %all-to-all-start.1 = ((f32[8,32,256]{2,0,1:T(8,128)}), f32[8,32,256]{2,0,1:T(8,128)S(1)}, u32[]{:S(2)}, u32[]{:S(2)}) async-start(f32[8,32,256]{2,0,1:T(8,128)} %copy.99), calls=%async_computation.1 | async-start | bytes 524288 | tf_op jit(solution)/shard_map/all_to_all | solution.py:77
  81.7 7.4 %all-to-all-done.1 = f32[8,32,256]{2,0,1:T(8,128)S(1)} async-done(((f32[8,32,256]{2,0,1:T(8,128)}), f32[8,32,256]{2,0,1:T(8,128)S(1)}, u32[]{:S(2)}, u32[]{:S(2)}) %all-to-all-start.1) | async-done | bytes 262176 | tf_op jit(solution)/shard_map/all_to_all | solution.py:77
  89.1 2.6 copy.101
  91.7 27.4 %scatter_fusion = f32[8,16384]{0,1:T(8,128)} fusion(f32[8,16384]{0,1:T(8,128)} %copy.100, s32[8192]{0:T(1024)S(1)} %bitcast.120, f32[8192,8]{1,0:T(8,128)} %copy.101), kind=kCustom, calls=%fused_computation.5 | custom fusion | bytes 819200 | tf_op jit(solution)/shard_map/scatter | solution.py:85
  119.1 12.3 %slice_sqrt_fusion = (f32[1,16384]{0,1:T(8,128)S(1)}, f32[16384]{0:T(1024)S(1)}) fusion(f32[8,16384]{0,1:T(8,128)} %scatter_fusion), kind=kLoop, calls=%fused_computation.44 | loop fusion | bytes 262144 | tf_op jit(solution)/shard_map/sqrt | solution.py:88
  131.4 4.4 %pad_maximum_fusion = f32[5,16384]{0,1:T(8,128)} fusion(f32[1,16384]{0,1:T(8,128)S(1)} %get-tuple-element.149, f32[4,16384]{0,1:T(8,128)S(1)} %bitcast.99), kind=kLoop, calls=%fused_computation.46 | loop fusion | flops 81920 | bytes 655360 | tf_op jit(solution)/shard_map/concatenate | solution.py:88
  135.8 4.1 %gather_fusion.2 = f32[256,5]{1,0:T(8,128)S(1)} fusion(f32[5,16384]{0,1:T(8,128)} %pad_maximum_fusion, s32[1024]{0:T(1024)S(1)} %pad_clamp_fusion.1), kind=kCustom, calls=%fused_computation.3 | custom fusion | bytes 11264 | tf_op jit(solution)/shard_map/gather | solution.py:92
  140.0 14.2 %gather_fusion.1 = f32[4096,5]{1,0:T(8,128)S(1)} fusion(f32[5,16384]{0,1:T(8,128)} %pad_maximum_fusion, s32[4096]{0:T(1024)S(1)} %bitcast_clamp_fusion), kind=kCustom, calls=%fused_computation.2 | custom fusion | bytes 180224 | tf_op jit(solution)/shard_map/gather | solution.py:91
  154.9 4.1 %collective-permute-start = (f32[5,1152]{1,0:T(8,128)S(1)}, f32[5,1152]{1,0:T(8,128)S(1)}, u32[]{:S(2)}, u32[]{:S(2)}) collective-permute-start(f32[5,1152]{1,0:T(8,128)S(1)} %concatenate.31), channel_id=1, source_target_pairs={{32,0},{64,32},{96,64},{128,96},{160,128},{192,160},{224,192},{256... | collective-permute-start | bytes 69128 | tf_op jit(solution)/shard_map/ppermute | solution.py:20
  161.0 5.1 %collective-permute-done.1 = f32[5,1152]{1,0:T(8,128)S(1)} collective-permute-done((f32[5,1152]{1,0:T(8,128)S(1)}, f32[5,1152]{1,0:T(8,128)S(1)}, u32[]{:S(2)}, u32[]{:S(2)}) %collective-permute-start.1) | collective-permute-done | bytes 23072 | tf_op jit(solution)/shard_map/ppermute | solution.py:20
  166.2 2.9 collective-permute-start.2
  169.2 5.7 %copy.104 = f32[5,16384]{1,0:T(8,128)S(1)} copy(f32[5,16384]{0,1:T(8,128)} %pad_maximum_fusion) | data formatting | bytes 655360 | tf_op jit(solution)/shard_map/concatenate | solution.py:88
  177.3 5.1 %collective-permute-done.3 = f32[5,1152]{1,0:T(8,128)S(1)} collective-permute-done((f32[5,1152]{1,0:T(8,128)S(1)}, f32[5,1152]{1,0:T(8,128)S(1)}, u32[]{:S(2)}, u32[]{:S(2)}) %collective-permute-start.3) | collective-permute-done | bytes 23072 | tf_op jit(solution)/shard_map/ppermute | solution.py:20
  182.5 132.0 %while.12 = (s32[]{:T(128)}, f32[16,2,8,128]{3,2,1,0:T(8,128)}, s32[16,24,2048]{2,1,0:T(8,128)}, s32[16,24]{1,0:T(8,128)S(1)}, f32[5,162,128]{2,0,1:T(8,128)S(1)...) while((s32[]{:T(128)}, f32[16,2,8,128]{3,2,1,0:T(8,128)}, ...), condition=%wide.region_7.8_spmd, body=%wide.region_3.7_spmd.sunk | while | flops 9450194 | bytes 2365079 | solution.py:138
  187.8 2.3 fusion.30
  196.0 2.3 fusion.30
  204.3 2.3 fusion.30
  212.5 2.3 fusion.30
  220.8 2.3 fusion.30
  229.0 2.3 fusion.30
  237.3 2.3 fusion.30
  245.5 2.3 fusion.30
  278.6 2.3 fusion.30
  315.5 4.7 %copy.106 = f32[2,16,8,128]{0,3,2,1:T(8,128)} copy(f32[2,16,8,128]{3,2,0,1:T(8,128)S(1)} %multiply_bitcast_fusion) | data formatting | bytes 262144 | tf_op jit(solution)/shard_map/mul | solution.py:142
  320.2 19.5 %slice_add_fusion = (f32[2,16384]{0,1:T(8,128)}, f32[2,16384]{0,1:T(8,128)}) fusion(f32[8,16384]{0,1:T(8,128)} %scatter_fusion, f32[16384]{0:T(1024)S(1)} %get-tuple-element.150, f32[2,16,8,128]{0,3,2,1:T(8,128)} %copy.106), kind=kLoop, calls=%fused_computation.42 | loop fusion | flops 131072 | bytes 720896 | tf_op jit(solution)/shard_map/add | solution.py:143
  339.7 5.9 %copy.108 = f32[2,16384]{1,0:T(2,128)} copy(f32[2,16384]{0,1:T(8,128)} %get-tuple-element.135) | data formatting | bytes 262144
  345.5 5.9 %copy.107 = f32[2,16384]{1,0:T(2,128)} copy(f32[2,16384]{0,1:T(8,128)} %get-tuple-element.136) | data formatting | bytes 262144
  (576 shorter events, 109.8 us)
Async XLA Ops:
  19.2 55.0 %all-to-all-start = ((s32[1,32,256]{2,0,1:T(1,128)}), s32[1,32,256]{2,0,1:T(1,128)S(1)}, u32[]{:S(2)}, u32[]{:S(2)}) async-start(s32[1,32,256]{2,0,1:T(1,128)} %bitcast.18), calls=%async_computation | async-start | bytes 65536 | tf_op jit(solution)/shard_map/all_to_all | solution.py:84
  74.2 14.9 %all-to-all-start.1 = ((f32[8,32,256]{2,0,1:T(8,128)}), f32[8,32,256]{2,0,1:T(8,128)S(1)}, u32[]{:S(2)}, u32[]{:S(2)}) async-start(f32[8,32,256]{2,0,1:T(8,128)} %copy.99), calls=%async_computation.1 | async-start | bytes 524288 | tf_op jit(solution)/shard_map/all_to_all | solution.py:77
  119.1 12.3 %copy-start = (f32[8,16384]{0,1:T(8,128)S(1)}, f32[8,16384]{0,1:T(8,128)}, u32[]{:S(2)}) copy-start(f32[8,16384]{0,1:T(8,128)} %scatter_fusion) | copy-start | bytes 1572868
  135.8 33.4 %copy-start.1 = (s32[384]{0:T(512)S(1)}, s32[384]{0:T(512)}, u32[]{:S(2)}) copy-start(s32[384]{0:T(512)} %param.24) | copy-start | bytes 4612
  154.9 6.1 %collective-permute-start = (f32[5,1152]{1,0:T(8,128)S(1)}, f32[5,1152]{1,0:T(8,128)S(1)}, u32[]{:S(2)}, u32[]{:S(2)}) collective-permute-start(f32[5,1152]{1,0:T(8,128)S(1)} %concatenate.31), channel_id=1, source_target_pairs={{32,0},{64,32},{96,64},{128,96},{160,128},{192,160},{224,192},{256... | collective-permute-start | bytes 69128 | tf_op jit(solution)/shard_map/ppermute | solution.py:20
  159.0 7.1 %collective-permute-start.1 = (f32[5,1152]{1,0:T(8,128)S(1)}, f32[5,1152]{1,0:T(8,128)S(1)}, u32[]{:S(2)}, u32[]{:S(2)}) collective-permute-start(f32[5,1152]{1,0:T(8,128)S(1)} %concatenate.32), channel_id=1, source_target_pairs={{0,32},{32,64},{64,96},{96,128},{128,160},{160,192},{192,224},{224... | collective-permute-start | bytes 69128 | tf_op jit(solution)/shard_map/ppermute | solution.py:20
  166.2 10.9 %collective-permute-start.2 = (f32[5,1152]{1,0:T(8,128)S(1)}, f32[5,1152]{1,0:T(8,128)S(1)}, u32[]{:S(2)}, u32[]{:S(2)}) collective-permute-start(f32[5,1152]{1,0:T(8,128)S(1)} %concatenate.33), channel_id=1, source_target_pairs={{1,0},{2,1},{3,2},{4,3},{5,4},{6,5},{7,6},{8,7},{9,8},{10,9},{11,1... | collective-permute-start | bytes 69128 | tf_op jit(solution)/shard_map/ppermute | solution.py:20
  175.0 7.4 %collective-permute-start.3 = (f32[5,1152]{1,0:T(8,128)S(1)}, f32[5,1152]{1,0:T(8,128)S(1)}, u32[]{:S(2)}, u32[]{:S(2)}) collective-permute-start(f32[5,1152]{1,0:T(8,128)S(1)} %concatenate.34), channel_id=1, source_target_pairs={{0,1},{1,2},{2,3},{3,4},{4,5},{5,6},{6,7},{7,8},{8,9},{9,10},{10,1... | collective-permute-start | bytes 69128 | tf_op jit(solution)/shard_map/ppermute | solution.py:20
where the time goes:
time: 353 us; the launch traced here: 351 us
  local copies, waits for them, and re-layouts  227 us (64%)
  other arithmetic  66.7 us (19%)
  starting transfers between devices  26 us (7%)
  waiting for transfers between devices  17.6 us (5%)
  loops' own time  13.2 us (4%)
    reduce_sum x16, other arithmetic, tile_forces(): push_x = jnp.sum(weight * sep_x, axis=2) * target[4]  37.1 us
    scatter x1, local copies, waits for them, and re-layouts, body(): empty.at[:, move_slot].set(ledger_item[:, move_rows])  35.8 us
    unnamed x7, local copies, waits for them, and re-layouts  28 us
    scatter x1, local copies, waits for them, and re-layouts, body(): ledger_item = ledger_item.at[:, placed[0]].set(arrived, mode='drop')  27.4 us
    dynamic_slice x32, local copies, waits for them, and re-layouts, body(): lax.map(group_push, (jnp.arange(groups, dtype=jnp.int32), source_groups,...  24.7 us
    add x1, other arithmetic, body(): front_rows[2:4] + SHIFT_STEP_SIZE * speeds_after_update  19.5 us
    reshape x32, local copies, waits for them, and re-layouts, unpack(): rows_words = bond_words.reshape(lead + (BLOCK, BLOCK // 8))  15.5 us
    gather x2, local copies, waits for them, and re-layouts, body(): edge_out = carried_message_content[:, edge_rows]  14.8 us
  transfers between devices with their start and end apart: 6, of which 3 were waited for; matrix products, arithmetic and copies ran while one was open for 15% of the time, Pallas kernels for 0%

commit v1 on v0

v1 whole, which is shorter than its diff:
```python
import functools

import jax
import jax.numpy as jnp
from jax import lax
from jax.experimental import pallas as pl
from jax.experimental.pallas import tpu as pltpu
from jax.sharding import PartitionSpec as P

F32 = jnp.float32
BF16 = jnp.bfloat16
I32 = jnp.int32

LANES = 128
PER_BLOCK = 3
NEAR_FLOOR = 0.5
BOND_COEFFICIENT = 0.005
SHIFT_STEP_SIZE = 0.5

PARTS = 3
SEND_ROWS = 24
SLOTS = 256
UNROLL = 4
VMEM_LIMIT = 56 * 1024 * 1024


def passed_along(block, axis, distance):
    devices = range(lax.axis_size(axis))
    route = [(i - distance, i) for i in devices if i - distance in devices]
    return lax.ppermute(block, axis, route)


def split(x):
    parts = []
    for _ in range(PARTS):
        part = x.astype(BF16)
        parts.append(part)
        x = x - part.astype(F32)
    return parts


def iota(shape, dim):
    return lax.broadcasted_iota(I32, shape, dim)


def ones_where(mask):
    return jnp.where(mask, 1.0, 0.0).astype(BF16)


def lookup_table(table, comp, x):
    for s, part in enumerate(split(x.T)):
        table[comp * LANES : (comp + 1) * LANES, s * LANES : (s + 1) * LANES] = part


def looked_up(table, comps, index):
    width = index.shape[1]
    high = ones_where(iota((LANES, width), 0) == (index >> 7))
    low = iota((LANES, width), 0) == (index & 127)
    found = jnp.dot(table[...], jnp.concatenate([high] * PARTS, 0), preferred_element_type=F32)
    return [
        jnp.sum(jnp.where(low, found[c * LANES : (c + 1) * LANES], 0.0), axis=0, keepdims=True)
        for c in range(comps)
    ]


def two_rows(ref, first):
    return jnp.concatenate([ref[pl.ds(first, 1), :], ref[pl.ds(first + 1, 1), :]], 1)


NT = (((1,), (1,)), ((), ()))


def send_kernel(pos, dis, vel, sti, den, rows, slots, news, out, table, spread, total):
    for c, ref in enumerate((pos, dis, vel)):
        for d in range(2):
            lookup_table(table, 2 * c + d, ref[pl.ds(d, LANES, stride=2), :])
    lookup_table(table, 6, sti[...])
    lookup_table(table, 7, den[...])
    total[...] = jnp.zeros_like(total)
    owners = out.shape[0] // SEND_ROWS

    @pl.loop(0, rows.shape[0] // 2)
    def _(k):
        index = two_rows(rows, 2 * k)
        slot = two_rows(slots, 2 * k)
        new = two_rows(news, 2 * k)
        values = looked_up(table, 8, index)
        values.append((new + 1).astype(F32))
        here = iota((owners, SLOTS), 0) == (slot >> 8)
        for c, value in enumerate(values):
            for s, part in enumerate(split(value)):
                at = (s * 9 + c) * owners
                spread[at : at + owners, :] = jnp.where(here, part.astype(F32), 0.0).astype(BF16)
        place = ones_where(iota((SLOTS, SLOTS), 0) == (slot & 255))
        total[...] += lax.dot_general(spread[...], place, NT, preferred_element_type=F32)

    out[...] = jnp.zeros_like(out)
    for c in range(9):
        value = total[c * owners : (c + 1) * owners, :]
        for s in range(1, PARTS):
            value = value + total[(s * 9 + c) * owners : (s * 9 + c + 1) * owners, :]
        out[pl.ds(2 * c, owners, stride=SEND_ROWS), :] = value[:, :LANES]
        out[pl.ds(2 * c + 1, owners, stride=SEND_ROWS), :] = value[:, LANES:]


def receive_kernel(
    got, pos, dis, vel, sti, den, edge_rows, corner_rows, record, *rest
):
    bundles, (table, spread, place, total) = rest[:4], rest[4:]
    owners = got.shape[0] // SEND_ROWS
    batch = place.shape[1] // SLOTS
    total[...] = jnp.zeros_like(total)

    @pl.loop(0, owners // batch)
    def _(k):
        for i in range(batch):
            first = (k * batch + i) * SEND_ROWS
            at_lanes = slice(i * SLOTS, (i + 1) * SLOTS)
            row = two_rows(got, first + 16).astype(I32) - 1
            here = iota((64, SLOTS), 0) == (row >> 8)
            for c in range(8):
                for s, part in enumerate(split(two_rows(got, first + 2 * c))):
                    at = (s * 8 + c) * 64
                    spread[at : at + 64, at_lanes] = jnp.where(
                        here, part.astype(F32), 0.0
                    ).astype(BF16)
            place[:, at_lanes] = ones_where(iota((256, SLOTS), 0) == (row & 255))
        total[...] += lax.dot_general(spread[...], place[...], NT, preferred_element_type=F32)

    def arrived(c):
        value = total[c * 64 : (c + 1) * 64, :]
        for s in range(1, PARTS):
            value = value + total[(s * 8 + c) * 64 : (s * 8 + c + 1) * 64, :]
        return value

    moved = arrived(6) > 0.25
    for c in range(8):
        value = arrived(c)
        for half in range(2):
            if c < 6:
                ref = (pos, dis, vel)[c // 2]
                kept = ref[pl.ds(2 * half + c % 2, 64, stride=4), :]
            else:
                kept = (sti, den)[c - 6][pl.ds(half, 64, stride=2), :]
            lanes = slice(half * LANES, (half + 1) * LANES)
            chosen = jnp.where(moved[:, lanes], value[:, lanes], kept)
            if c == 6:
                chosen = jnp.sqrt(chosen)
            record[pl.ds(c * LANES + half, 64, stride=2), :] = chosen
    for c, source in enumerate((0, 1, 2, 3, 6)):
        lookup_table(table, c, record[source * LANES : (source + 1) * LANES, :])
    for edge, bundle in zip((0, 3, 1, 2), bundles):

        @pl.loop(0, edge_rows.shape[1] // 256)
        def _(q):
            index = edge_rows[edge : edge + 1, pl.ds(pl.multiple_of(q * 256, 256), 256)]
            for c, value in enumerate(looked_up(table, 5, index)):
                bundle[pl.ds(c * 8 + 2 * q, 1), :] = value[:, :LANES]
                bundle[pl.ds(c * 8 + 2 * q + 1, 1), :] = value[:, LANES:]

    corners = corner_rows[...]
    index = jnp.concatenate([corners[i : i + 1, :] for i in range(4)], 1)
    for b in range(2):
        bundles[b][40:48, :] = jnp.zeros((8, LANES), F32)
    for c, value in enumerate(looked_up(table, 5, index)):
        bundles[0][40 + c : 41 + c, :] = value[:, :LANES]
        bundles[1][40 + c : 41 + c, :] = value[:, LANES:]


def list_kernel(source, near_tile, near_source, far_tile, far_source, counts):
    tiles = source.shape[0]

    def step(t, carry):
        near, far = carry
        src = source[t]
        near_tile[near] = t
        near_source[near] = src
        far_tile[far] = t
        far_source[far] = src
        is_near = (src < LANES).astype(I32)
        return near + is_near, far + 1 - is_near

    near, far = lax.fori_loop(0, tiles, step, (jnp.int32(0), jnp.int32(0)))
    for i in range(UNROLL):
        near_tile[near + i] = tiles
        near_source[near + i] = 0
        far_tile[far + i] = tiles
        far_source[far + i] = LANES
    counts[0] = (near + UNROLL - 1) // UNROLL
    counts[1] = (far + UNROLL - 1) // UNROLL


def expand_targets(record, targets):
    parts = [
        jnp.concatenate(split(record[c * LANES : (c + 1) * LANES, :]), 1) for c in range(4)
    ]
    values = jnp.concatenate(parts, 0)
    for r in range(0, 16, 2):
        shape = (LANES, 2 * LANES)
        lane = iota(shape, 1)
        chosen = ones_where(iota(shape, 0) == 8 * r + lane // 16)
        spread = jnp.dot(
            values, jnp.concatenate([chosen] * PARTS, 0), preferred_element_type=F32
        )
        for c in range(4):
            for half in range(2):
                targets[pl.ds(c * 16 + r + half, LANES, stride=64), :] = spread[
                    c * LANES : (c + 1) * LANES, half * LANES : (half + 1) * LANES
                ]


def expand_sources(arrays, sources):
    count = arrays[0].shape[0]
    values = jnp.concatenate([jnp.concatenate(split(a), 1) for a in arrays], 0)
    for b in range(0, 8, 2):
        shape = (LANES, 2 * LANES)
        lane = iota(shape, 1)
        chosen = ones_where(iota(shape, 0) == 8 * (lane % 16) + b + lane // LANES)
        spread = jnp.dot(
            values, jnp.concatenate([chosen] * PARTS, 0), preferred_element_type=F32
        )
        for c in range(5):
            for half in range(2):
                value = spread[c * count : (c + 1) * count, half * LANES : (half + 1) * LANES]
                if c == 4:
                    value = value * (2.0 ** -(b + half))
                sources[pl.ds(c * 8 + b + half, count, stride=40), :] = value


def tile_loop(steps, tile_ids, tile_sources, first_block, words, targets, sources, pushed):
    tiles = words.shape[0] // 16

    def one_tile(position):
        tile = tile_ids[position]
        base = (tile_sources[position] - first_block) * 40
        known = jnp.minimum(tile, tiles - 1)
        word = words[pl.ds((known >> 3) * LANES + (known & 7), 16, stride=8), :]
        block = pl.multiple_of(((known * 43691) >> 17) * 64, 64)
        tx, ty, tu, tv = (targets[pl.ds(block + 16 * c, 16), :] for c in range(4))
        push_x = push_y = None
        for b in range(8):
            sx, sy, su, sv, root = (
                sources[pl.ds(base + 8 * c + b, 1), :] for c in range(5)
            )
            sep_x, sep_y = sx - tx, sy - ty
            rel_x, rel_y = su - tu, sv - tv
            square = sep_x * sep_x + sep_y * sep_y
            inverse = lax.rsqrt(jnp.maximum(square, NEAR_FLOOR * NEAR_FLOOR))
            intact = (word & (1 << b)).astype(F32)
            weight = (
                (sep_x * rel_x + sep_y * rel_y)
                * (inverse * inverse)
                * (inverse * root)
                * intact
            )
            more_x, more_y = weight * sep_x, weight * sep_y
            push_x = more_x if b == 0 else push_x + more_x
            push_y = more_y if b == 0 else push_y + more_y
        return tile, push_x, push_y

    @pl.loop(0, steps)
    def _(step):
        for tile, push_x, push_y in [one_tile(step * UNROLL + i) for i in range(UNROLL)]:
            at = pl.multiple_of(tile * 32, 32)
            pushed[pl.ds(at, 16), :] = push_x
            pushed[pl.ds(at + 16, 16), :] = push_y


def gathered_force(pushed, comp, blocks):
    stride = 32 * PER_BLOCK
    total = None
    for r in range(16):
        value = None
        for k in range(PER_BLOCK):
            part = pushed[pl.ds(32 * k + 16 * comp + r, blocks, stride=stride), :]
            value = part if value is None else value + part
        shape = (LANES, LANES)
        chosen = ones_where(iota(shape, 1) == 8 * r + iota(shape, 0) // 16)
        more = jnp.dot(
            jnp.concatenate(split(value), 1),
            jnp.concatenate([chosen] * PARTS, 0),
            preferred_element_type=F32,
        )
        total = more if total is None else total + more
    return total


def near_kernel(tile_ids, tile_sources, counts, record, words, force, targets, sources, pushed):
    pushed[...] = jnp.zeros_like(pushed)
    expand_targets(record, targets)
    expand_sources(
        [record[c * LANES : (c + 1) * LANES, :] for c in (0, 1, 2, 3, 6)], sources
    )
    tile_loop(counts[0], tile_ids, tile_sources, 0, words, targets, sources, pushed)
    for d in range(2):
        force[d * LANES : (d + 1) * LANES, :] = gathered_force(pushed, d, LANES)


def far_kernel(
    tile_ids, tile_sources, counts, record, words, force, x_low, x_high, y_low, y_high,
    speeds, offsets, targets, sources, pushed
):
    pushed[...] = jnp.zeros_like(pushed)
    expand_targets(record, targets)
    halo = []
    left = iota((1, LANES), 1) < 64
    for c in range(5):
        edges = [ref[8 * c : 8 * c + 8, :] for ref in (x_low, y_low, y_high, x_high)]
        corners = [
            jnp.where(left, y_low[r + c : r + c + 1, :], y_high[r + c : r + c + 1, :])
            for r in (40, 48)
        ]
        halo.append(jnp.concatenate(edges + corners + [jnp.zeros((6, LANES), F32)], 0))
    expand_sources(halo, sources)
    tile_loop(counts[1], tile_ids, tile_sources, LANES, words, targets, sources, pushed)
    root = record[6 * LANES : 7 * LANES, :]
    density = record[7 * LANES : 8 * LANES, :]
    for d in range(2):
        total = force[d * LANES : (d + 1) * LANES, :] + gathered_force(pushed, d, LANES)
        speed = record[(4 + d) * LANES : (5 + d) * LANES, :] + (
            BOND_COEFFICIENT * (total * root) / density
        )
        speeds[pl.ds(d, LANES, stride=2), :] = speed
        offsets[pl.ds(d, LANES, stride=2), :] = (
            record[(2 + d) * LANES : (3 + d) * LANES, :] + SHIFT_STEP_SIZE * speed
        )


VM = pl.BlockSpec(memory_space=pltpu.VMEM)
SM = pl.BlockSpec(memory_space=pltpu.SMEM)


def call(kernel, in_specs, outs, scratch, name, flops=0, moved=0):
    return pl.pallas_call(
        kernel,
        name=name,
        in_specs=in_specs,
        out_specs=[spec for spec, _, _ in outs],
        out_shape=[jax.ShapeDtypeStruct(shape, dtype) for _, shape, dtype in outs],
        scratch_shapes=[pltpu.VMEM(shape, dtype) for shape, dtype in scratch],
        cost_estimate=pl.CostEstimate(flops=flops, bytes_accessed=moved, transcendentals=0),
        compiler_params=pltpu.CompilerParams(vmem_limit_bytes=VMEM_LIMIT),
    )


def pair_rows(x):
    return x.reshape(2, LANES, LANES).transpose(1, 0, 2).reshape(2 * LANES, LANES)


def unpair_rows(x):
    return x.reshape(LANES, 2, LANES).transpose(1, 0, 2).reshape(2, LANES * LANES)


def body(
    positions,
    displacement,
    velocity,
    stiffness,
    density,
    move_rows,
    move_slot,
    move_new,
    edge_rows,
    corner_rows,
    tile_src,
    bond_bits,
):
    owners = lax.axis_size("gy")
    tiles = tile_src.shape[0]
    state = (
        pair_rows(positions),
        pair_rows(displacement),
        pair_rows(velocity),
        stiffness.reshape(LANES, LANES),
        density.reshape(LANES, LANES),
    )
    moves = tuple(m.reshape(-1, LANES) for m in (move_rows, move_slot, move_new))
    words = (
        bond_bits.reshape(tiles // 8, 8, 16, LANES).transpose(0, 2, 1, 3).reshape(-1, LANES)
    )

    (outgoing,) = call(
        send_kernel,
        [VM] * 8,
        [(VM, (owners * SEND_ROWS, LANES), F32)],
        [
            ((8 * LANES, PARTS * LANES), BF16),
            ((PARTS * 9 * owners, SLOTS), BF16),
            ((PARTS * 9 * owners, SLOTS), F32),
        ],
        "send",
    )(*state, *moves)
    got = lax.all_to_all(
        outgoing.reshape(owners, SEND_ROWS, LANES), "gy", split_axis=0, concat_axis=0, tiled=True
    ).reshape(owners * SEND_ROWS, LANES)

    listed = tiles + UNROLL
    near_tile, near_source, far_tile, far_source, counts = call(
        list_kernel,
        [SM],
        [(SM, (listed,), I32)] * 4 + [(SM, (2,), I32)],
        [],
        "lists",
    )(tile_src)

    batch = 4
    record, x_low, x_high, y_low, y_high = call(
        receive_kernel,
        [VM] * 8,
        [(VM, (8 * LANES, LANES), F32)]
        + [(VM, (48, LANES), F32)] * 2
        + [(VM, (40, LANES), F32)] * 2,
        [
            ((5 * LANES, PARTS * LANES), BF16),
            ((PARTS * 8 * 64, batch * SLOTS), BF16),
            ((256, batch * SLOTS), BF16),
            ((PARTS * 8 * 64, 256), F32),
        ],
        "receive",
    )(got, *state, edge_rows, corner_rows)

    x_low = passed_along(x_low, "gx", -1)
    x_high = passed_along(x_high, "gx", 1)
    corners = [x_low[40:], x_high[40:]]
    y_low = passed_along(jnp.concatenate([y_low] + corners, 0), "gy", -1)
    y_high = passed_along(jnp.concatenate([y_high] + corners, 0), "gy", 1)

    (force,) = call(
        near_kernel,
        [SM] * 3 + [VM] * 2,
        [(VM, (2 * LANES, LANES), F32)],
        [
            ((64 * LANES, LANES), F32),
            ((40 * LANES, LANES), F32),
            ((32 * (tiles + 1), LANES), F32),
        ],
        "near",
        flops=10**9,
        moved=10**8,
    )(near_tile, near_source, counts, record, words)
    speeds, offsets = call(
        far_kernel,
        [SM] * 3 + [VM] * 7,
        [(VM, (2 * LANES, LANES), F32)] * 2,
        [
            ((64 * LANES, LANES), F32),
            ((40 * 40, LANES), F32),
            ((32 * (tiles + 1), LANES), F32),
        ],
        "far",
    )(far_tile, far_source, counts, record, words, force, x_low, x_high, y_low, y_high)
    return unpair_rows(speeds), unpair_rows(offsets)


def solution(mesh):
    placed = (
        P(None, ("gx", "gy")),
        P(None, ("gx", "gy")),
        P(None, ("gx", "gy")),
        P(("gx", "gy")),
        P(("gx", "gy")),
        P(("gx", "gy")),
        P(("gx", "gy")),
        P(("gx", "gy")),
        P(None, ("gx", "gy")),
        P(None, ("gx", "gy")),
        P(("gx", "gy")),
        P(("gx", "gy"), None),
    )
    return jax.shard_map(
        body,
        mesh=mesh,
        in_specs=placed,
        out_specs=(P(None, ("gx", "gy")), P(None, ("gx", "gy"))),
        check_vma=False,
    )
```

time: 353 us -> 118 us (0.33)
  the two profiles are of different devices: /device:TPU:392 before, /device:TPU:8 now
where the time goes in v1:
time: 118 us
  Pallas kernels  83.3 us (71%)
  blocking collectives  18.7 us (16%)
  starting transfers between devices  13.5 us (11%)
    pallas_call x1, Pallas kernels, body(): call(near_kernel, [SM] * 3 + [VM] * 2, [(VM, (2 * LANES, LANES), F32)], [...  30.4 us
    all_to_all x1, blocking collectives, body(): lax.all_to_all(outgoing.reshape(owners, SEND_ROWS, LANES), 'gy', split_ax...  18.7 us
    pallas_call x1, Pallas kernels, body(): call(far_kernel, [SM] * 3 + [VM] * 7, [(VM, (2 * LANES, LANES), F32)] * 2...  16.3 us
    pallas_call x1, Pallas kernels, body(): call(receive_kernel, [VM] * 8, [(VM, (8 * LANES, LANES), F32)] + [(VM, (4...  16.2 us
    pallas_call x1, Pallas kernels, body(): call(send_kernel, [VM] * 8, [(VM, (owners * SEND_ROWS, LANES), F32)], [((...  16.2 us
    ppermute x4, starting transfers between devices, passed_along(): return lax.ppermute(block, axis, route)  13.5 us
    pallas_call x1, Pallas kernels, body(): call(list_kernel, [SM], [(SM, (listed,), I32)] * 4 + [(SM, (2,), I32)], [...  4.21 us
  transfers between devices with their start and end apart: 4, of which 0 were waited for; matrix products, arithmetic and copies ran while one was open for 0% of the time, Pallas kernels for 29%

profile of v1, /device:TPU:8, one launch (start us, length us, event | category | flops | bytes accessed | tf_op | source)
XLA Modules:
  0.0 117.6 jit_solution(14075839035749435502)
XLA Ops:
  0.6 16.2 %send.1 = f32[768,128]{1,0:T(8,128)} custom-call(f32[256,128]{1,0:T(8,128)} %bitcast.41, f32[256,128]{1,0:T(8,128)} %bitcast.43, f32[256,128]{1,0:T(8,128)} %bitcast.45, f32[128,128]{1,0:T(8,128)} %bitcast.47, f32[128,128]{1,0:T(8,128)} %bitcast.49, s32[32,128]{1,0:T(8,128)} %bitcast.51, s32[32,128]{1,0:T(8,128)} %bitcast.52, s32[32,128]{1,0:T(8,128)} %bitcast.53), custom_call_target="tpu_custom_call" | custom-call | tf_op jit(solution)/shard_map/send/pallas_call | solution.py:382
  16.8 18.7 %all_to_all.5 = f32[32,24,128]{2,1,0:T(8,128)} all-to-all(f32[32,24,128]{2,1,0:T(8,128)} %bitcast.40), channel_id=1, replica_groups=mesh['gx'=16,'gy'=32] {'gy'}, dimensions={0} | all-to-all | bytes 786432 | tf_op jit(solution)/shard_map/all_to_all | solution.py:393
  35.5 16.2 %receive.1 = (f32[1024,128]{1,0:T(8,128)}, f32[48,128]{1,0:T(8,128)}, f32[48,128]{1,0:T(8,128)}, f32[40,128]{1,0:T(8,128)}, f32[40,128]{1,0:T(8,128)}) custom-call(f32[768,128]{1,0:T(8,128)} %bitcast.39, f32[256,128]{1,0:T(8,128)} %bitcast.42, f32[256,128]{1,0:T(8,128)} %bitcast.44, f32[256,128]{1,0:T(8,128)} %bitcast.46, f32[128,128]{1,0:T(8,128)} %bitcast.48, ...), custom_call_target="tpu_custom_call" | custom-call | tf_op jit(solution)/shard_map/receive/pallas_call | solution.py:407
  51.7 1.3 %collective-permute-start = (f32[48,128]{1,0:T(8,128)}, f32[48,128]{1,0:T(8,128)S(1)}, u32[]{:S(2)}, u32[]{:S(2)}) collective-permute-start(f32[48,128]{1,0:T(8,128)} %get-tuple-element.20), channel_id=1, source_target_pairs={{32,0},{64,32},{96,64},{128,96},{160,128},{192,160},{224,192},{256... | collective-permute-start | bytes 73736 | tf_op jit(solution)/shard_map/ppermute | solution.py:30
  53.0 4.5 %collective-permute-start.1 = (f32[48,128]{1,0:T(8,128)}, f32[48,128]{1,0:T(8,128)S(1)}, u32[]{:S(2)}, u32[]{:S(2)}) collective-permute-start(f32[48,128]{1,0:T(8,128)} %get-tuple-element.21), channel_id=1, source_target_pairs={{0,32},{32,64},{64,96},{96,128},{128,160},{160,192},{192,224},{224... | collective-permute-start | bytes 73736 | tf_op jit(solution)/shard_map/ppermute | solution.py:30
  57.6 4.2 %lists.1 = (s32[388]{0:T(512)}, s32[388]{0:T(512)}, s32[388]{0:T(512)}, s32[388]{0:T(512)}, s32[2]{0:T(128)}) custom-call(s32[384]{0:T(512)} %source.1), custom_call_target="tpu_custom_call" | custom-call | tf_op jit(solution)/shard_map/lists/pallas_call | solution.py:398
  61.8 0.0 collective-permute-done.x_low
  61.8 0.0 copy-start
  61.8 0.0 collective-permute-done.1.x_high
  61.8 0.0 copy-start.1
  61.8 0.8 pad_maximum_fusion
  62.6 2.0 %collective-permute-start.3 = (f32[56,128]{1,0:T(8,128)S(1)}, f32[56,128]{1,0:T(8,128)S(1)}, u32[]{:S(2)}, u32[]{:S(2)}) collective-permute-start(f32[56,128]{1,0:T(8,128)S(1)} %get-tuple-element.26), channel_id=1, source_target_pairs={{0,1},{1,2},{2,3},{3,4},{4,5},{5,6},{6,7},{7,8},{8,9},{9,10},{10,1... | collective-permute-start | bytes 86024 | tf_op jit(solution)/shard_map/ppermute | solution.py:30
  64.6 5.7 %collective-permute-start.2 = (f32[56,128]{1,0:T(8,128)S(1)}, f32[56,128]{1,0:T(8,128)S(1)}, u32[]{:S(2)}, u32[]{:S(2)}) collective-permute-start(f32[56,128]{1,0:T(8,128)S(1)} %get-tuple-element.27), channel_id=1, source_target_pairs={{1,0},{2,1},{3,2},{4,3},{5,4},{6,5},{7,6},{8,7},{9,8},{10,9},{11,1... | collective-permute-start | bytes 86024 | tf_op jit(solution)/shard_map/ppermute | solution.py:30
  70.3 30.4 %near.1.force = f32[256,128]{1,0:T(8,128)} custom-call(s32[388]{0:T(512)} %get-tuple-element.18.tile_ids, s32[388]{0:T(512)} %get-tuple-element.19.tile_sources, s32[2]{0:T(128)} %get-tuple-element.16.counts, f32[1024,128]{1,0:T(8,128)} %get-tuple-element.17.record, s32[6144,128]{1,0:T(8,128)} %bitcast.37), custom_call_target="tpu_custom_call" | custom-call | flops 1000000000 | bytes 100000000 | tf_op jit(solution)/shard_map/near/pallas_call | solution.py:428
  100.7 0.0 collective-permute-done.3.y_high
  100.7 0.0 copy-start.2
  100.7 0.0 collective-permute-done.2.y_low
  100.7 0.0 copy-start.3
  100.7 0.0 copy-done
  100.7 0.0 copy-done.1
  100.7 0.6 copy-done.2
  101.3 0.0 copy-done.3
  101.3 16.3 %far.1 = (f32[256,128]{1,0:T(8,128)}, f32[256,128]{1,0:T(8,128)}) custom-call(s32[388]{0:T(512)} %get-tuple-element.14.tile_ids, s32[388]{0:T(512)} %get-tuple-element.15.tile_sources, s32[2]{0:T(128)} %get-tuple-element.16.counts, f32[1024,128]{1,0:T(8,128)} %get-tuple-element.17.record, s32[6144,128]{1,0:T(8,128)} %bitcast.38, f32[256,128]{1,0:T(8,128)} %near.1.force, ...), custom_call_target="tpu_custom_call" | custom-call | tf_op jit(solution)/shard_map/far/pallas_call | solution.py:441
  (2 shorter events, 0.0 us)
Async XLA Ops:
  51.7 10.1 %collective-permute-start = (f32[48,128]{1,0:T(8,128)}, f32[48,128]{1,0:T(8,128)S(1)}, u32[]{:S(2)}, u32[]{:S(2)}) collective-permute-start(f32[48,128]{1,0:T(8,128)} %get-tuple-element.20), channel_id=1, source_target_pairs={{32,0},{64,32},{96,64},{128,96},{160,128},{192,160},{224,192},{256... | collective-permute-start | bytes 73736 | tf_op jit(solution)/shard_map/ppermute | solution.py:30
  53.0 8.8 %collective-permute-start.1 = (f32[48,128]{1,0:T(8,128)}, f32[48,128]{1,0:T(8,128)S(1)}, u32[]{:S(2)}, u32[]{:S(2)}) collective-permute-start(f32[48,128]{1,0:T(8,128)} %get-tuple-element.21), channel_id=1, source_target_pairs={{0,32},{32,64},{64,96},{96,128},{128,160},{160,192},{192,224},{224... | collective-permute-start | bytes 73736 | tf_op jit(solution)/shard_map/ppermute | solution.py:30
  61.8 38.9 %copy-start = (f32[48,128]{1,0:T(8,128)}, f32[48,128]{1,0:T(8,128)S(1)}, u32[]{:S(2)}) copy-start(f32[48,128]{1,0:T(8,128)S(1)} %collective-permute-done.x_low) | copy-start | bytes 73732
  61.8 38.9 %copy-start.1 = (f32[48,128]{1,0:T(8,128)}, f32[48,128]{1,0:T(8,128)S(1)}, u32[]{:S(2)}) copy-start(f32[48,128]{1,0:T(8,128)S(1)} %collective-permute-done.1.x_high) | copy-start | bytes 73732
  62.6 38.1 %collective-permute-start.3 = (f32[56,128]{1,0:T(8,128)S(1)}, f32[56,128]{1,0:T(8,128)S(1)}, u32[]{:S(2)}, u32[]{:S(2)}) collective-permute-start(f32[56,128]{1,0:T(8,128)S(1)} %get-tuple-element.26), channel_id=1, source_target_pairs={{0,1},{1,2},{2,3},{3,4},{4,5},{5,6},{6,7},{7,8},{8,9},{9,10},{10,1... | collective-permute-start | bytes 86024 | tf_op jit(solution)/shard_map/ppermute | solution.py:30
  64.6 36.1 %collective-permute-start.2 = (f32[56,128]{1,0:T(8,128)S(1)}, f32[56,128]{1,0:T(8,128)S(1)}, u32[]{:S(2)}, u32[]{:S(2)}) collective-permute-start(f32[56,128]{1,0:T(8,128)S(1)} %get-tuple-element.27), channel_id=1, source_target_pairs={{1,0},{2,1},{3,2},{4,3},{5,4},{6,5},{7,6},{8,7},{9,8},{10,9},{11,1... | collective-permute-start | bytes 86024 | tf_op jit(solution)/shard_map/ppermute | solution.py:30
  100.7 0.6 copy-start.2
  100.7 0.6 copy-start.3

commit v2 on v1

--- a/solution.py
+++ b/solution.py
@@ -21,6 +21,7 @@
 SEND_ROWS = 24
 SLOTS = 256
 UNROLL = 4
+TARGET_ROWS = 72
 VMEM_LIMIT = 56 * 1024 * 1024
 
 
@@ -48,17 +49,19 @@
 
 
 def lookup_table(table, comp, x):
-    for s, part in enumerate(split(x.T)):
-        table[comp * LANES : (comp + 1) * LANES, s * LANES : (s + 1) * LANES] = part
+    turned = x.T
+    turned = jnp.concatenate([turned[:64], turned[64:]], 1)
+    for s, part in enumerate(split(turned)):
+        table[comp * 64 : (comp + 1) * 64, s * 256 : (s + 1) * 256] = part
 
 
 def looked_up(table, comps, index):
     width = index.shape[1]
-    high = ones_where(iota((LANES, width), 0) == (index >> 7))
-    low = iota((LANES, width), 0) == (index & 127)
+    high = ones_where(iota((256, width), 0) == ((index >> 7) + ((index & 64) << 1)))
+    low = iota((64, width), 0) == (index & 63)
     found = jnp.dot(table[...], jnp.concatenate([high] * PARTS, 0), preferred_element_type=F32)
     return [
-        jnp.sum(jnp.where(low, found[c * LANES : (c + 1) * LANES], 0.0), axis=0, keepdims=True)
+        jnp.sum(jnp.where(low, found[c * 64 : (c + 1) * 64], 0.0), axis=0, keepdims=True)
         for c in range(comps)
     ]
 
@@ -70,7 +73,11 @@
 NT = (((1,), (1,)), ((), ()))
 
 
-def send_kernel(pos, dis, vel, sti, den, rows, slots, news, out, table, spread, total):
+def send_kernel(
+    source, pos, dis, vel, sti, den, rows, slots, news,
+    out, near_tile, near_source, far_tile, far_source, counts,
+    table, spread, place, total
+):
     for c, ref in enumerate((pos, dis, vel)):
         for d in range(2):
             lookup_table(table, 2 * c + d, ref[pl.ds(d, LANES, stride=2), :])
@@ -78,21 +85,48 @@
     lookup_table(table, 7, den[...])
     total[...] = jnp.zeros_like(total)
     owners = out.shape[0] // SEND_ROWS
-
-    @pl.loop(0, rows.shape[0] // 2)
-    def _(k):
-        index = two_rows(rows, 2 * k)
-        slot = two_rows(slots, 2 * k)
-        new = two_rows(news, 2 * k)
-        values = looked_up(table, 8, index)
-        values.append((new + 1).astype(F32))
-        here = iota((owners, SLOTS), 0) == (slot >> 8)
-        for c, value in enumerate(values):
-            for s, part in enumerate(split(value)):
-                at = (s * 9 + c) * owners
-                spread[at : at + owners, :] = jnp.where(here, part.astype(F32), 0.0).astype(BF16)
-        place = ones_where(iota((SLOTS, SLOTS), 0) == (slot & 255))
-        total[...] += lax.dot_general(spread[...], place, NT, preferred_element_type=F32)
+    tiles = source.shape[0]
+    batch = place.shape[1] // SLOTS
+    steps = rows.shape[0] // 2 // batch
+
+    def step(k, carry):
+        near, far = carry
+        for i in range(tiles // steps):
+            tile = k * (tiles // steps) + i
+            src = source[tile]
+            near_tile[near] = tile
+            near_source[near] = src
+            far_tile[far] = tile
+            far_source[far] = src
+            is_near = (src < LANES).astype(I32)
+            near, far = near + is_near, far + 1 - is_near
+        for i in range(batch):
+            first = 2 * (k * batch + i)
+            at_lanes = slice(i * SLOTS, (i + 1) * SLOTS)
+            index = two_rows(rows, first)
+            slot = two_rows(slots, first)
+            new = two_rows(news, first)
+            values = looked_up(table, 8, index)
+            values.append((new + 1).astype(F32))
+            here = iota((owners, SLOTS), 0) == (slot >> 8)
+            for c, value in enumerate(values):
+                for s, part in enumerate(split(value)):
+                    at = (s * 9 + c) * owners
+                    spread[at : at + owners, at_lanes] = jnp.where(
+                        here, part.astype(F32), 0.0
+                    ).astype(BF16)
+            place[:, at_lanes] = ones_where(iota((SLOTS, SLOTS), 0) == (slot & 255))
+        total[...] += lax.dot_general(spread[...], place[...], NT, preferred_element_type=F32)
+        return near, far
+
+    near, far = lax.fori_loop(0, steps, step, (jnp.int32(0), jnp.int32(0)))
+    for i in range(UNROLL):
+        near_tile[near + i] = tiles
+        near_source[near + i] = 0
+        far_tile[far + i] = tiles
+        far_source[far + i] = LANES
+    counts[0] = (near + UNROLL - 1) // UNROLL
+    counts[1] = (far + UNROLL - 1) // UNROLL
 
     out[...] = jnp.zeros_like(out)
     for c in range(9):
@@ -149,10 +183,9 @@
             record[pl.ds(c * LANES + half, 64, stride=2), :] = chosen
     for c, source in enumerate((0, 1, 2, 3, 6)):
         lookup_table(table, c, record[source * LANES : (source + 1) * LANES, :])
-    for edge, bundle in zip((0, 3, 1, 2), bundles):
-
-        @pl.loop(0, edge_rows.shape[1] // 256)
-        def _(q):
+    @pl.loop(0, edge_rows.shape[1] // 256)
+    def _(q):
+        for edge, bundle in zip((0, 3, 1, 2), bundles):
             index = edge_rows[edge : edge + 1, pl.ds(pl.multiple_of(q * 256, 256), 256)]
             for c, value in enumerate(looked_up(table, 5, index)):
                 bundle[pl.ds(c * 8 + 2 * q, 1), :] = value[:, :LANES]
@@ -165,29 +198,6 @@
     for c, value in enumerate(looked_up(table, 5, index)):
         bundles[0][40 + c : 41 + c, :] = value[:, :LANES]
         bundles[1][40 + c : 41 + c, :] = value[:, LANES:]
-
-
-def list_kernel(source, near_tile, near_source, far_tile, far_source, counts):
-    tiles = source.shape[0]
-
-    def step(t, carry):
-        near, far = carry
-        src = source[t]
-        near_tile[near] = t
-        near_source[near] = src
-        far_tile[far] = t
-        far_source[far] = src
-        is_near = (src < LANES).astype(I32)
-        return near + is_near, far + 1 - is_near
-
-    near, far = lax.fori_loop(0, tiles, step, (jnp.int32(0), jnp.int32(0)))
-    for i in range(UNROLL):
-        near_tile[near + i] = tiles
-        near_source[near + i] = 0
-        far_tile[far + i] = tiles
-        far_source[far + i] = LANES
-    counts[0] = (near + UNROLL - 1) // UNROLL
-    counts[1] = (far + UNROLL - 1) // UNROLL
 
 
 def expand_targets(record, targets):
@@ -204,7 +214,7 @@
         )
         for c in range(4):
             for half in range(2):
-                targets[pl.ds(c * 16 + r + half, LANES, stride=64), :] = spread[
+                targets[pl.ds(c * 16 + r + half, LANES, stride=TARGET_ROWS), :] = spread[
                     c * LANES : (c + 1) * LANES, half * LANES : (half + 1) * LANES
                 ]
 
@@ -235,7 +245,7 @@
         base = (tile_sources[position] - first_block) * 40
         known = jnp.minimum(tile, tiles - 1)
         word = words[pl.ds((known >> 3) * LANES + (known & 7), 16, stride=8), :]
-        block = pl.multiple_of(((known * 43691) >> 17) * 64, 64)
+        block = pl.multiple_of(((known * 43691) >> 17) * TARGET_ROWS, 8)
         tx, ty, tu, tv = (targets[pl.ds(block + 16 * c, 16), :] for c in range(4))
         push_x = push_y = None
         for b in range(8):
@@ -266,40 +276,48 @@
             pushed[pl.ds(at + 16, 16), :] = push_y
 
 
-def gathered_force(pushed, comp, blocks):
-    stride = 32 * PER_BLOCK
-    total = None
-    for r in range(16):
-        value = None
-        for k in range(PER_BLOCK):
-            part = pushed[pl.ds(32 * k + 16 * comp + r, blocks, stride=stride), :]
-            value = part if value is None else value + part
-        shape = (LANES, LANES)
-        chosen = ones_where(iota(shape, 1) == 8 * r + iota(shape, 0) // 16)
-        more = jnp.dot(
-            jnp.concatenate(split(value), 1),
-            jnp.concatenate([chosen] * PARTS, 0),
-            preferred_element_type=F32,
-        )
-        total = more if total is None else total + more
-    return total
-
-
-def near_kernel(tile_ids, tile_sources, counts, record, words, force, targets, sources, pushed):
+def gather_force(pushed, force):
+    many = 64
+    shape = (LANES, LANES)
+    chosen = ones_where(iota(shape, 0) // 16 == iota(shape, 1) % 8)
+    chosen = jnp.concatenate([chosen] * PARTS, 0)
+    own = iota((16, LANES), 1) // 8 == iota((16, LANES), 0)
+
+    @pl.loop(0, force.shape[0] // 2 // many)
+    def _(group):
+        values = []
+        for i in range(many):
+            at = pl.multiple_of((group * many + i) * 32 * PER_BLOCK, 32)
+            value = pushed[pl.ds(at, 32), :]
+            for k in range(1, PER_BLOCK):
+                value = value + pushed[pl.ds(at + 32 * k, 32), :]
+            values.append(jnp.concatenate(split(value), 1))
+        sums = jnp.dot(jnp.concatenate(values, 0), chosen, preferred_element_type=F32)
+        sums = jnp.where(own[None], sums.reshape(2 * many, 16, LANES), 0.0)
+        force[pl.ds(pl.multiple_of(group * 2 * many, 2 * many), 2 * many), :] = jnp.sum(sums, axis=1)
+
+
+def near_kernel(
+    tile_ids, tile_sources, counts, record, bonds, force, words, sem, targets, sources, pushed
+):
+    copy = pltpu.make_async_copy(bonds, words, sem)
+    copy.start()
     pushed[...] = jnp.zeros_like(pushed)
     expand_targets(record, targets)
     expand_sources(
         [record[c * LANES : (c + 1) * LANES, :] for c in (0, 1, 2, 3, 6)], sources
     )
+    copy.wait()
     tile_loop(counts[0], tile_ids, tile_sources, 0, words, targets, sources, pushed)
-    for d in range(2):
-        force[d * LANES : (d + 1) * LANES, :] = gathered_force(pushed, d, LANES)
+    gather_force(pushed, force)
 
 
 def far_kernel(
-    tile_ids, tile_sources, counts, record, words, force, x_low, x_high, y_low, y_high,
-    speeds, offsets, targets, sources, pushed
+    tile_ids, tile_sources, counts, record, bonds, force, x_low, x_high, y_low, y_high,
+    speeds, offsets, words, sem, more, targets, sources, pushed
 ):
+    copy = pltpu.make_async_copy(bonds, words, sem)
+    copy.start()
     pushed[...] = jnp.zeros_like(pushed)
     expand_targets(record, targets)
     halo = []
@@ -312,22 +330,26 @@
         ]
         halo.append(jnp.concatenate(edges + corners + [jnp.zeros((6, LANES), F32)], 0))
     expand_sources(halo, sources)
+    copy.wait()
     tile_loop(counts[1], tile_ids, tile_sources, LANES, words, targets, sources, pushed)
+    gather_force(pushed, more)
     root = record[6 * LANES : 7 * LANES, :]
     density = record[7 * LANES : 8 * LANES, :]
     for d in range(2):
-        total = force[d * LANES : (d + 1) * LANES, :] + gathered_force(pushed, d, LANES)
+        at = pl.ds(d, LANES, stride=2)
+        total = force[at, :] + more[at, :]
         speed = record[(4 + d) * LANES : (5 + d) * LANES, :] + (
             BOND_COEFFICIENT * (total * root) / density
         )
-        speeds[pl.ds(d, LANES, stride=2), :] = speed
-        offsets[pl.ds(d, LANES, stride=2), :] = (
+        speeds[at, :] = speed
+        offsets[at, :] = (
             record[(2 + d) * LANES : (3 + d) * LANES, :] + SHIFT_STEP_SIZE * speed
         )
 
 
 VM = pl.BlockSpec(memory_space=pltpu.VMEM)
 SM = pl.BlockSpec(memory_space=pltpu.SMEM)
+HBM = pl.BlockSpec(memory_space=pl.ANY)
 
 
 def call(kernel, in_specs, outs, scratch, name, flops=0, moved=0):
@@ -337,7 +359,9 @@
         in_specs=in_specs,
         out_specs=[spec for spec, _, _ in outs],
         out_shape=[jax.ShapeDtypeStruct(shape, dtype) for _, shape, dtype in outs],
-        scratch_shapes=[pltpu.VMEM(shape, dtype) for shape, dtype in scratch],
+        scratch_shapes=[
+            pltpu.SemaphoreType.DMA if not entry else pltpu.VMEM(*entry) for entry in scratch
+        ],
         cost_estimate=pl.CostEstimate(flops=flops, bytes_accessed=moved, transcendentals=0),
         compiler_params=pltpu.CompilerParams(vmem_limit_bytes=VMEM_LIMIT),
     )
@@ -379,31 +403,26 @@
         bond_bits.reshape(tiles // 8, 8, 16, LANES).transpose(0, 2, 1, 3).reshape(-1, LANES)
     )
 
-    (outgoing,) = call(
+    batch = 4
+    listed = tiles + UNROLL
+    outgoing, near_tile, near_source, far_tile, far_source, counts = call(
         send_kernel,
-        [VM] * 8,
-        [(VM, (owners * SEND_ROWS, LANES), F32)],
+        [SM] + [VM] * 8,
+        [(VM, (owners * SEND_ROWS, LANES), F32)]
+        + [(SM, (listed,), I32)] * 4
+        + [(SM, (2,), I32)],
         [
-            ((8 * LANES, PARTS * LANES), BF16),
-            ((PARTS * 9 * owners, SLOTS), BF16),
+            ((8 * 64, PARTS * 256), BF16),
+            ((PARTS * 9 * owners, batch * SLOTS), BF16),
+            ((SLOTS, batch * SLOTS), BF16),
             ((PARTS * 9 * owners, SLOTS), F32),
         ],
         "send",
-    )(*state, *moves)
+    )(tile_src, *state, *moves)
     got = lax.all_to_all(
         outgoing.reshape(owners, SEND_ROWS, LANES), "gy", split_axis=0, concat_axis=0, tiled=True
     ).reshape(owners * SEND_ROWS, LANES)
 
-    listed = tiles + UNROLL
-    near_tile, near_source, far_tile, far_source, counts = call(
-        list_kernel,
-        [SM],
-        [(SM, (listed,), I32)] * 4 + [(SM, (2,), I32)],
-        [],
-        "lists",
-    )(tile_src)
-
-    batch = 4
     record, x_low, x_high, y_low, y_high = call(
         receive_kernel,
         [VM] * 8,
@@ -411,7 +430,7 @@
         + [(VM, (48, LANES), F32)] * 2
         + [(VM, (40, LANES), F32)] * 2,
         [
-            ((5 * LANES, PARTS * LANES), BF16),
+            ((5 * 64, PARTS * 256), BF16),
             ((PARTS * 8 * 64, batch * SLOTS), BF16),
             ((256, batch * SLOTS), BF16),
             ((PARTS * 8 * 64, 256), F32),
@@ -427,10 +446,12 @@
 
     (force,) = call(
         near_kernel,
-        [SM] * 3 + [VM] * 2,
+        [SM] * 3 + [VM, HBM],
         [(VM, (2 * LANES, LANES), F32)],
         [
-            ((64 * LANES, LANES), F32),
+            (words.shape, I32),
+            (),
+            ((TARGET_ROWS * LANES, LANES), F32),
             ((40 * LANES, LANES), F32),
             ((32 * (tiles + 1), LANES), F32),
         ],
@@ -440,10 +461,13 @@
     )(near_tile, near_source, counts, record, words)
     speeds, offsets = call(
         far_kernel,
-        [SM] * 3 + [VM] * 7,
+        [SM] * 3 + [VM, HBM] + [VM] * 5,
         [(VM, (2 * LANES, LANES), F32)] * 2,
         [
-            ((64 * LANES, LANES), F32),
+            (words.shape, I32),
+            (),
+            ((2 * LANES, LANES), F32),
+            ((TARGET_ROWS * LANES, LANES), F32),
             ((40 * 40, LANES), F32),
             ((32 * (tiles + 1), LANES), F32),
         ],

time: 118 us -> 92 us (0.78)
  the two profiles are of different devices: /device:TPU:8 before, /device:TPU:392 now
where the time goes in v2:
time: 92 us; the launch traced here: 91.4 us
  Pallas kernels  54.2 us (59%)
  blocking collectives  16.2 us (18%)
  starting transfers between devices  13.7 us (15%)
  waiting for transfers between devices  5.19 us (6%)
    pallas_call x1, Pallas kernels, body(): call(near_kernel, [SM] * 3 + [VM, HBM], [(VM, (2 * LANES, LANES), F32)],...  20.7 us
    all_to_all x1, blocking collectives, body(): lax.all_to_all(outgoing.reshape(owners, SEND_ROWS, LANES), 'gy', split_ax...  16.2 us
    ppermute x4, starting transfers between devices, passed_along(): return lax.ppermute(block, axis, route)  13.7 us
    pallas_call x1, Pallas kernels, body(): call(receive_kernel, [VM] * 8, [(VM, (8 * LANES, LANES), F32)] + [(VM, (4...  13.6 us
    pallas_call x1, Pallas kernels, body(): call(far_kernel, [SM] * 3 + [VM, HBM] + [VM] * 5, [(VM, (2 * LANES, LANES...  9.97 us
    pallas_call x1, Pallas kernels, body(): call(send_kernel, [SM] + [VM] * 8, [(VM, (owners * SEND_ROWS, LANES), F32...  9.93 us
    ppermute x4, waiting for transfers between devices, passed_along(): return lax.ppermute(block, axis, route)  5.19 us
  transfers between devices with their start and end apart: 4, of which 1 were waited for; matrix products, arithmetic and copies ran while one was open for 0% of the time, Pallas kernels for 23%

profile of v2, /device:TPU:392, one launch (start us, length us, event | category | flops | bytes accessed | tf_op | source)
XLA Modules:
  0.0 91.4 jit_solution(1255350010612725014)
XLA Ops:
  0.6 9.9 %send.1 = (f32[768,128]{1,0:T(8,128)}, s32[388]{0:T(512)}, s32[388]{0:T(512)}, s32[388]{0:T(512)}, s32[388]{0:T(512)}, /*index=5*/s32[2]{0:T(128)}) custom-call(s32[384]{0:T(512)} %source.1, f32[256,128]{1,0:T(8,128)} %bitcast.40, f32[256,128]{1,0:T(8,128)} %bitcast.42, f32[256,128]{1,0:T(8,128)} %bitcast.44, f32[128,128]{1,0:T(8,128)} %bitcast.47, ...), custom_call_target="tpu_custom_call" | custom-call | tf_op jit(solution)/shard_map/send/pallas_call | solution.py:408
  10.6 16.2 %all_to_all.5 = f32[32,24,128]{2,1,0:T(8,128)} all-to-all(f32[32,24,128]{2,1,0:T(8,128)} %bitcast.46), channel_id=1, replica_groups=mesh['gx'=16,'gy'=32] {'gy'}, dimensions={0} | all-to-all | bytes 786432 | tf_op jit(solution)/shard_map/all_to_all | solution.py:422
  26.8 13.6 %receive.1 = (f32[1024,128]{1,0:T(8,128)}, f32[48,128]{1,0:T(8,128)}, f32[48,128]{1,0:T(8,128)}, f32[40,128]{1,0:T(8,128)}, f32[40,128]{1,0:T(8,128)}) custom-call(f32[768,128]{1,0:T(8,128)} %bitcast.39, f32[256,128]{1,0:T(8,128)} %bitcast.41, f32[256,128]{1,0:T(8,128)} %bitcast.43, f32[256,128]{1,0:T(8,128)} %bitcast.45, f32[128,128]{1,0:T(8,128)} %bitcast.48, ...), custom_call_target="tpu_custom_call" | custom-call | tf_op jit(solution)/shard_map/receive/pallas_call | solution.py:426
  40.4 4.1 %collective-permute-start = (f32[48,128]{1,0:T(8,128)}, f32[48,128]{1,0:T(8,128)S(1)}, u32[]{:S(2)}, u32[]{:S(2)}) collective-permute-start(f32[48,128]{1,0:T(8,128)} %get-tuple-element.22), channel_id=1, source_target_pairs={{32,0},{64,32},{96,64},{128,96},{160,128},{192,160},{224,192},{256... | collective-permute-start | bytes 73736 | tf_op jit(solution)/shard_map/ppermute | solution.py:31
  44.6 1.9 %collective-permute-start.1 = (f32[48,128]{1,0:T(8,128)}, f32[48,128]{1,0:T(8,128)S(1)}, u32[]{:S(2)}, u32[]{:S(2)}) collective-permute-start(f32[48,128]{1,0:T(8,128)} %get-tuple-element.23), channel_id=1, source_target_pairs={{0,32},{32,64},{64,96},{96,128},{128,160},{160,192},{192,224},{224... | collective-permute-start | bytes 73736 | tf_op jit(solution)/shard_map/ppermute | solution.py:31
  46.5 0.0 collective-permute-done.x_low
  46.5 0.0 copy-start
  46.5 5.2 %collective-permute-done.1.x_high = f32[48,128]{1,0:T(8,128)S(1)} collective-permute-done((f32[48,128]{1,0:T(8,128)}, f32[48,128]{1,0:T(8,128)S(1)}, u32[]{:S(2)}, u32[]{:S(2)}) %collective-permute-start.1) | collective-permute-done | bytes 24608 | tf_op jit(solution)/shard_map/ppermute | solution.py:31
  51.7 0.0 copy-start.1
  51.7 0.8 pad_maximum_fusion
  52.5 1.9 %collective-permute-start.3 = (f32[56,128]{1,0:T(8,128)S(1)}, f32[56,128]{1,0:T(8,128)S(1)}, u32[]{:S(2)}, u32[]{:S(2)}) collective-permute-start(f32[56,128]{1,0:T(8,128)S(1)} %get-tuple-element.28), channel_id=1, source_target_pairs={{0,1},{1,2},{2,3},{3,4},{4,5},{5,6},{6,7},{7,8},{8,9},{9,10},{10,1... | collective-permute-start | bytes 86024 | tf_op jit(solution)/shard_map/ppermute | solution.py:31
  54.4 5.8 %collective-permute-start.2 = (f32[56,128]{1,0:T(8,128)S(1)}, f32[56,128]{1,0:T(8,128)S(1)}, u32[]{:S(2)}, u32[]{:S(2)}) collective-permute-start(f32[56,128]{1,0:T(8,128)S(1)} %get-tuple-element.29), channel_id=1, source_target_pairs={{1,0},{2,1},{3,2},{4,3},{5,4},{6,5},{7,6},{8,7},{9,8},{10,9},{11,1... | collective-permute-start | bytes 86024 | tf_op jit(solution)/shard_map/ppermute | solution.py:31
  60.1 20.7 %near.1.force = f32[256,128]{1,0:T(8,128)} custom-call(s32[388]{0:T(512)} %get-tuple-element.20.tile_ids, s32[388]{0:T(512)} %get-tuple-element.21.tile_sources, s32[2]{0:T(128)} %get-tuple-element.17.counts, f32[1024,128]{1,0:T(8,128)} %get-tuple-element.19.record, s32[6144,128]{1,0:T(8,128)} %bitcast.37), custom_call_target="tpu_custom_call" | custom-call | flops 1000000000 | bytes 100000000 | tf_op jit(solution)/shard_map/near/pallas_call | solution.py:447
  80.8 0.0 collective-permute-done.3.y_high
  80.8 0.0 copy-start.2
  80.8 0.0 collective-permute-done.2.y_low
  80.9 0.0 copy-start.3
  80.9 0.0 copy-done
  80.9 0.0 copy-done.1
  80.9 0.5 copy-done.2
  81.4 0.0 copy-done.3
  81.5 10.0 %far.1 = (f32[256,128]{1,0:T(8,128)}, f32[256,128]{1,0:T(8,128)}) custom-call(s32[388]{0:T(512)} %get-tuple-element.15.tile_ids, s32[388]{0:T(512)} %get-tuple-element.16.tile_sources, s32[2]{0:T(128)} %get-tuple-element.17.counts, f32[1024,128]{1,0:T(8,128)} %get-tuple-element.19.record, s32[6144,128]{1,0:T(8,128)} %bitcast.38, f32[256,128]{1,0:T(8,128)} %near.1.force, ...), custom_call_target="tpu_custom_call" | custom-call | tf_op jit(solution)/shard_map/far/pallas_call | solution.py:462
  (2 shorter events, 0.0 us)
Async XLA Ops:
  40.4 6.1 %collective-permute-start = (f32[48,128]{1,0:T(8,128)}, f32[48,128]{1,0:T(8,128)S(1)}, u32[]{:S(2)}, u32[]{:S(2)}) collective-permute-start(f32[48,128]{1,0:T(8,128)} %get-tuple-element.22), channel_id=1, source_target_pairs={{32,0},{64,32},{96,64},{128,96},{160,128},{192,160},{224,192},{256... | collective-permute-start | bytes 73736 | tf_op jit(solution)/shard_map/ppermute | solution.py:31
  44.6 7.1 %collective-permute-start.1 = (f32[48,128]{1,0:T(8,128)}, f32[48,128]{1,0:T(8,128)S(1)}, u32[]{:S(2)}, u32[]{:S(2)}) collective-permute-start(f32[48,128]{1,0:T(8,128)} %get-tuple-element.23), channel_id=1, source_target_pairs={{0,32},{32,64},{64,96},{96,128},{128,160},{160,192},{192,224},{224... | collective-permute-start | bytes 73736 | tf_op jit(solution)/shard_map/ppermute | solution.py:31
  46.5 34.4 %copy-start = (f32[48,128]{1,0:T(8,128)}, f32[48,128]{1,0:T(8,128)S(1)}, u32[]{:S(2)}) copy-start(f32[48,128]{1,0:T(8,128)S(1)} %collective-permute-done.x_low) | copy-start | bytes 73732
  51.7 29.2 %copy-start.1 = (f32[48,128]{1,0:T(8,128)}, f32[48,128]{1,0:T(8,128)S(1)}, u32[]{:S(2)}) copy-start(f32[48,128]{1,0:T(8,128)S(1)} %collective-permute-done.1.x_high) | copy-start | bytes 73732
  52.5 28.4 %collective-permute-start.3 = (f32[56,128]{1,0:T(8,128)S(1)}, f32[56,128]{1,0:T(8,128)S(1)}, u32[]{:S(2)}, u32[]{:S(2)}) collective-permute-start(f32[56,128]{1,0:T(8,128)S(1)} %get-tuple-element.28), channel_id=1, source_target_pairs={{0,1},{1,2},{2,3},{3,4},{4,5},{5,6},{6,7},{7,8},{8,9},{9,10},{10,1... | collective-permute-start | bytes 86024 | tf_op jit(solution)/shard_map/ppermute | solution.py:31
  54.4 26.5 %collective-permute-start.2 = (f32[56,128]{1,0:T(8,128)S(1)}, f32[56,128]{1,0:T(8,128)S(1)}, u32[]{:S(2)}, u32[]{:S(2)}) collective-permute-start(f32[56,128]{1,0:T(8,128)S(1)} %get-tuple-element.29), channel_id=1, source_target_pairs={{1,0},{2,1},{3,2},{4,3},{5,4},{6,5},{7,6},{8,7},{9,8},{10,9},{11,1... | collective-permute-start | bytes 86024 | tf_op jit(solution)/shard_map/ppermute | solution.py:31
  80.8 0.6 copy-start.2
  80.9 0.6 copy-start.3

commit v3 on v2

--- a/solution.py
+++ b/solution.py
@@ -18,11 +18,12 @@
 SHIFT_STEP_SIZE = 0.5
 
 PARTS = 3
+MOVED_PARTS = (3, 3, 3, 3, 2, 2, 2, 2, 2)
 SEND_ROWS = 24
 SLOTS = 256
 UNROLL = 4
 TARGET_ROWS = 72
-VMEM_LIMIT = 56 * 1024 * 1024
+MIB = 1024 * 1024
 
 
 def passed_along(block, axis, distance):
@@ -31,15 +32,34 @@
     return lax.ppermute(block, axis, route)
 
 
-def split(x):
+def split(x, count=PARTS):
     parts = []
-    for _ in range(PARTS):
+    for _ in range(count):
         part = x.astype(BF16)
         parts.append(part)
         x = x - part.astype(F32)
     return parts
 
 
+def first_part(c):
+    return sum(MOVED_PARTS[:c])
+
+
+def added_parts(total, c, rows):
+    at = first_part(c) * rows
+    value = total[at : at + rows, :]
+    for s in range(1, MOVED_PARTS[c]):
+        value = value + total[at + s * rows : at + (s + 1) * rows, :]
+    return value
+
+
+def copied(pairs, sem):
+    copies = [pltpu.make_async_copy(a, b, sem.at[i]) for i, (a, b) in enumerate(pairs)]
+    for copy in copies:
+        copy.start()
+    return copies
+
+
 def iota(shape, dim):
     return lax.broadcasted_iota(I32, shape, dim)
 
@@ -51,19 +71,24 @@
 def lookup_table(table, comp, x):
     turned = x.T
     turned = jnp.concatenate([turned[:64], turned[64:]], 1)
-    for s, part in enumerate(split(turned)):
+    for s, part in enumerate(split(turned, table.shape[1] // 256)):
         table[comp * 64 : (comp + 1) * 64, s * 256 : (s + 1) * 256] = part
 
 
-def looked_up(table, comps, index):
+def looked_up(tables, index):
     width = index.shape[1]
     high = ones_where(iota((256, width), 0) == ((index >> 7) + ((index & 64) << 1)))
     low = iota((64, width), 0) == (index & 63)
-    found = jnp.dot(table[...], jnp.concatenate([high] * PARTS, 0), preferred_element_type=F32)
-    return [
-        jnp.sum(jnp.where(low, found[c * 64 : (c + 1) * 64], 0.0), axis=0, keepdims=True)
-        for c in range(comps)
-    ]
+    values = []
+    for table in tables:
+        parts = table.shape[1] // 256
+        found = jnp.dot(
+            table[...], jnp.concatenate([high] * parts, 0), preferred_element_type=F32
+        )
+        for c in range(table.shape[0] // 64):
+            chosen = jnp.where(low, found[c * 64 : (c + 1) * 64], 0.0)
+            values.append(jnp.sum(chosen, axis=0, keepdims=True))
+    return values
 
 
 def two_rows(ref, first):
@@ -73,16 +98,21 @@
 NT = (((1,), (1,)), ((), ()))
 
 
-def send_kernel(
-    source, pos, dis, vel, sti, den, rows, slots, news,
-    out, near_tile, near_source, far_tile, far_source, counts,
-    table, spread, place, total
-):
-    for c, ref in enumerate((pos, dis, vel)):
+def send_kernel(*refs):
+    arguments, refs = refs[:9], refs[9:]
+    (out, near_tile, near_source, far_tile, far_source, counts), refs = refs[:6], refs[6:]
+    held, (sem, table, coarse, spread, place, total) = refs[:9], refs[9:]
+    copies = copied(zip(arguments, held), sem)
+    source, pos, dis, vel, sti, den, rows, slots, news = held
+    for copy in copies:
+        copy.wait()
+    for c, ref in enumerate((pos, dis)):
         for d in range(2):
             lookup_table(table, 2 * c + d, ref[pl.ds(d, LANES, stride=2), :])
-    lookup_table(table, 6, sti[...])
-    lookup_table(table, 7, den[...])
+    for d in range(2):
+        lookup_table(coarse, d, vel[pl.ds(d, LANES, stride=2), :])
+    lookup_table(coarse, 2, sti[...])
+    lookup_table(coarse, 3, den[...])
     total[...] = jnp.zeros_like(total)
     owners = out.shape[0] // SEND_ROWS
     tiles = source.shape[0]
@@ -106,12 +136,12 @@
             index = two_rows(rows, first)
             slot = two_rows(slots, first)
             new = two_rows(news, first)
-            values = looked_up(table, 8, index)
+            values = looked_up((table, coarse), index)
             values.append((new + 1).astype(F32))
             here = iota((owners, SLOTS), 0) == (slot >> 8)
             for c, value in enumerate(values):
-                for s, part in enumerate(split(value)):
-                    at = (s * 9 + c) * owners
+                for s, part in enumerate(split(value, MOVED_PARTS[c])):
+                    at = (first_part(c) + s) * owners
                     spread[at : at + owners, at_lanes] = jnp.where(
                         here, part.astype(F32), 0.0
                     ).astype(BF16)
@@ -130,17 +160,17 @@
 
     out[...] = jnp.zeros_like(out)
     for c in range(9):
-        value = total[c * owners : (c + 1) * owners, :]
-        for s in range(1, PARTS):
-            value = value + total[(s * 9 + c) * owners : (s * 9 + c + 1) * owners, :]
+        value = added_parts(total, c, owners)
         out[pl.ds(2 * c, owners, stride=SEND_ROWS), :] = value[:, :LANES]
         out[pl.ds(2 * c + 1, owners, stride=SEND_ROWS), :] = value[:, LANES:]
 
 
-def receive_kernel(
-    got, pos, dis, vel, sti, den, edge_rows, corner_rows, record, *rest
-):
-    bundles, (table, spread, place, total) = rest[:4], rest[4:]
+def receive_kernel(got, *refs):
+    arguments, refs = refs[:7], refs[7:]
+    (record, table, x_low, x_high), refs = refs[:4], refs[4:]
+    held, (sem, spread, place, total) = refs[:7], refs[7:]
+    copies = copied(zip(arguments, held), sem)
+    pos, dis, vel, sti, den, edge_rows, corner_rows = held
     owners = got.shape[0] // SEND_ROWS
     batch = place.shape[1] // SLOTS
     total[...] = jnp.zeros_like(total)
@@ -153,23 +183,20 @@
             row = two_rows(got, first + 16).astype(I32) - 1
             here = iota((64, SLOTS), 0) == (row >> 8)
             for c in range(8):
-                for s, part in enumerate(split(two_rows(got, first + 2 * c))):
-                    at = (s * 8 + c) * 64
+                value = two_rows(got, first + 2 * c)
+                for s, part in enumerate(split(value, MOVED_PARTS[c])):
+                    at = (first_part(c) + s) * 64
                     spread[at : at + 64, at_lanes] = jnp.where(
                         here, part.astype(F32), 0.0
                     ).astype(BF16)
             place[:, at_lanes] = ones_where(iota((256, SLOTS), 0) == (row & 255))
         total[...] += lax.dot_general(spread[...], place[...], NT, preferred_element_type=F32)
 
-    def arrived(c):
-        value = total[c * 64 : (c + 1) * 64, :]
-        for s in range(1, PARTS):
-            value = value + total[(s * 8 + c) * 64 : (s * 8 + c + 1) * 64, :]
-        return value
-
-    moved = arrived(6) > 0.25
+    for copy in copies:
+        copy.wait()
+    moved = added_parts(total, 6, 64) > 0.25
     for c in range(8):
-        value = arrived(c)
+        value = added_parts(total, c, 64)
         for half in range(2):
             if c < 6:
                 ref = (pos, dis, vel)[c // 2]
@@ -183,21 +210,38 @@
             record[pl.ds(c * LANES + half, 64, stride=2), :] = chosen
     for c, source in enumerate((0, 1, 2, 3, 6)):
         lookup_table(table, c, record[source * LANES : (source + 1) * LANES, :])
-    @pl.loop(0, edge_rows.shape[1] // 256)
-    def _(q):
-        for edge, bundle in zip((0, 3, 1, 2), bundles):
-            index = edge_rows[edge : edge + 1, pl.ds(pl.multiple_of(q * 256, 256), 256)]
-            for c, value in enumerate(looked_up(table, 5, index)):
-                bundle[pl.ds(c * 8 + 2 * q, 1), :] = value[:, :LANES]
-                bundle[pl.ds(c * 8 + 2 * q + 1, 1), :] = value[:, LANES:]
-
+    look_up_edges(table, edge_rows, ((0, x_low), (3, x_high)))
     corners = corner_rows[...]
     index = jnp.concatenate([corners[i : i + 1, :] for i in range(4)], 1)
-    for b in range(2):
-        bundles[b][40:48, :] = jnp.zeros((8, LANES), F32)
-    for c, value in enumerate(looked_up(table, 5, index)):
-        bundles[0][40 + c : 41 + c, :] = value[:, :LANES]
-        bundles[1][40 + c : 41 + c, :] = value[:, LANES:]
+    for ref in (x_low, x_high):
+        ref[40:48, :] = jnp.zeros((8, LANES), F32)
+    for c, value in enumerate(looked_up((table,), index)):
+        x_low[40 + c : 41 + c, :] = value[:, :LANES]
+        x_high[40 + c : 41 + c, :] = value[:, LANES:]
+
+
+def look_up_edges(table, edge_rows, bundles):
+    half = edge_rows.shape[1] // 512
+
+    @pl.loop(0, half)
+    def _(q):
+        for edge, bundle in bundles:
+            for i in range(2):
+                at = q + i * half
+                index = edge_rows[edge : edge + 1, pl.ds(pl.multiple_of(at * 256, 256), 256)]
+                for c, value in enumerate(looked_up((table,), index)):
+                    bundle[pl.ds(c * 8 + 2 * at, 1), :] = value[:, :LANES]
+                    bundle[pl.ds(c * 8 + 2 * at + 1, 1), :] = value[:, LANES:]
+
+
+def expand_kernel(record, table, rows, y_low, y_high, targets, sources, edge_rows, sem):
+    copies = copied([(rows, edge_rows)], sem)
+    expand_targets(record, targets)
+    expand_sources(
+        [record[c * LANES : (c + 1) * LANES, :] for c in (0, 1, 2, 3, 6)], sources
+    )
+    copies[0].wait()
+    look_up_edges(table, edge_rows, ((1, y_low), (2, y_high)))
 
 
 def expand_targets(record, targets):
@@ -280,7 +324,7 @@
     many = 64
     shape = (LANES, LANES)
     chosen = ones_where(iota(shape, 0) // 16 == iota(shape, 1) % 8)
-    chosen = jnp.concatenate([chosen] * PARTS, 0)
+    chosen = jnp.concatenate([chosen] * 2, 0)
     own = iota((16, LANES), 1) // 8 == iota((16, LANES), 0)
 
     @pl.loop(0, force.shape[0] // 2 // many)
@@ -291,35 +335,25 @@
             value = pushed[pl.ds(at, 32), :]
             for k in range(1, PER_BLOCK):
                 value = value + pushed[pl.ds(at + 32 * k, 32), :]
-            values.append(jnp.concatenate(split(value), 1))
+            values.append(jnp.concatenate(split(value, 2), 1))
         sums = jnp.dot(jnp.concatenate(values, 0), chosen, preferred_element_type=F32)
         sums = jnp.where(own[None], sums.reshape(2 * many, 16, LANES), 0.0)
         force[pl.ds(pl.multiple_of(group * 2 * many, 2 * many), 2 * many), :] = jnp.sum(sums, axis=1)
 
 
 def near_kernel(
-    tile_ids, tile_sources, counts, record, bonds, force, words, sem, targets, sources, pushed
+    tile_ids, tile_sources, counts, targets, sources, words, force, pushed
 ):
-    copy = pltpu.make_async_copy(bonds, words, sem)
-    copy.start()
     pushed[...] = jnp.zeros_like(pushed)
-    expand_targets(record, targets)
-    expand_sources(
-        [record[c * LANES : (c + 1) * LANES, :] for c in (0, 1, 2, 3, 6)], sources
-    )
-    copy.wait()
     tile_loop(counts[0], tile_ids, tile_sources, 0, words, targets, sources, pushed)
     gather_force(pushed, force)
 
 
 def far_kernel(
-    tile_ids, tile_sources, counts, record, bonds, force, x_low, x_high, y_low, y_high,
-    speeds, offsets, words, sem, more, targets, sources, pushed
+    tile_ids, tile_sources, counts, record, targets, words, force,
+    x_low, x_high, y_low, y_high, speeds, offsets, more, sources, pushed
 ):
-    copy = pltpu.make_async_copy(bonds, words, sem)
-    copy.start()
     pushed[...] = jnp.zeros_like(pushed)
-    expand_targets(record, targets)
     halo = []
     left = iota((1, LANES), 1) < 64
     for c in range(5):
@@ -330,7 +364,6 @@
         ]
         halo.append(jnp.concatenate(edges + corners + [jnp.zeros((6, LANES), F32)], 0))
     expand_sources(halo, sources)
-    copy.wait()
     tile_loop(counts[1], tile_ids, tile_sources, LANES, words, targets, sources, pushed)
     gather_force(pushed, more)
     root = record[6 * LANES : 7 * LANES, :]
@@ -349,10 +382,10 @@
 
 VM = pl.BlockSpec(memory_space=pltpu.VMEM)
 SM = pl.BlockSpec(memory_space=pltpu.SMEM)
-HBM = pl.BlockSpec(memory_space=pl.ANY)
-
-
-def call(kernel, in_specs, outs, scratch, name, flops=0, moved=0):
+HBM = pl.BlockSpec(memory_space=pltpu.HBM)
+
+
+def call(kernel, in_specs, outs, scratch, name, vmem, flops=0, moved=0):
     return pl.pallas_call(
         kernel,
         name=name,
@@ -360,10 +393,13 @@
         out_specs=[spec for spec, _, _ in outs],
         out_shape=[jax.ShapeDtypeStruct(shape, dtype) for _, shape, dtype in outs],
         scratch_shapes=[
-            pltpu.SemaphoreType.DMA if not entry else pltpu.VMEM(*entry) for entry in scratch
+            pltpu.SemaphoreType.DMA(entry)
+            if len(entry) == 1
+            else (entry[2] if len(entry) == 3 else pltpu.VMEM)(*entry[:2])
+            for entry in scratch
         ],
         cost_estimate=pl.CostEstimate(flops=flops, bytes_accessed=moved, transcendentals=0),
-        compiler_params=pltpu.CompilerParams(vmem_limit_bytes=VMEM_LIMIT),
+        compiler_params=pltpu.CompilerParams(vmem_limit_bytes=vmem * MIB),
     )
 
 
@@ -402,77 +438,101 @@
     words = (
         bond_bits.reshape(tiles // 8, 8, 16, LANES).transpose(0, 2, 1, 3).reshape(-1, LANES)
     )
+    state, moves, (edge_rows, corner_rows, tile_src) = (
+        tuple(pltpu.with_memory_space_constraint(x, pltpu.HBM) for x in group)
+        for group in (state, moves, (edge_rows, corner_rows, tile_src))
+    )
 
     batch = 4
     listed = tiles + UNROLL
+    moved_parts = first_part(9)
+    held = [((2 * LANES, LANES), F32)] * 3 + [((LANES, LANES), F32)] * 2
     outgoing, near_tile, near_source, far_tile, far_source, counts = call(
         send_kernel,
-        [SM] + [VM] * 8,
+        [HBM] * 9,
         [(VM, (owners * SEND_ROWS, LANES), F32)]
         + [(SM, (listed,), I32)] * 4
         + [(SM, (2,), I32)],
-        [
-            ((8 * 64, PARTS * 256), BF16),
-            ((PARTS * 9 * owners, batch * SLOTS), BF16),
+        [(tile_src.shape, I32, pltpu.SMEM)]
+        + held
+        + [(moves[0].shape, I32)] * 3
+        + [
+            (9,),
+            ((4 * 64, 3 * 256), BF16),
+            ((4 * 64, 2 * 256), BF16),
+            ((moved_parts * owners, batch * SLOTS), BF16),
             ((SLOTS, batch * SLOTS), BF16),
-            ((PARTS * 9 * owners, SLOTS), F32),
+            ((moved_parts * owners, SLOTS), F32),
         ],
         "send",
+        16,
     )(tile_src, *state, *moves)
     got = lax.all_to_all(
         outgoing.reshape(owners, SEND_ROWS, LANES), "gy", split_axis=0, concat_axis=0, tiled=True
     ).reshape(owners * SEND_ROWS, LANES)
 
-    record, x_low, x_high, y_low, y_high = call(
+    state_parts = first_part(8)
+    record, table, x_low, x_high = call(
         receive_kernel,
-        [VM] * 8,
-        [(VM, (8 * LANES, LANES), F32)]
-        + [(VM, (48, LANES), F32)] * 2
-        + [(VM, (40, LANES), F32)] * 2,
-        [
-            ((5 * 64, PARTS * 256), BF16),
-            ((PARTS * 8 * 64, batch * SLOTS), BF16),
+        [VM] + [HBM] * 7,
+        [(VM, (8 * LANES, LANES), F32), (VM, (5 * 64, PARTS * 256), BF16)]
+        + [(VM, (48, LANES), F32)] * 2,
+        held
+        + [
+            (edge_rows.shape, I32),
+            (corner_rows.shape, I32),
+            (7,),
+            ((state_parts * 64, batch * SLOTS), BF16),
             ((256, batch * SLOTS), BF16),
-            ((PARTS * 8 * 64, 256), F32),
+            ((state_parts * 64, 256), F32),
         ],
         "receive",
+        16,
     )(got, *state, edge_rows, corner_rows)
 
     x_low = passed_along(x_low, "gx", -1)
     x_high = passed_along(x_high, "gx", 1)
+    y_low, y_high, targets, sources = call(
+        expand_kernel,
+        [VM, VM, HBM],
+        [(VM, (40, LANES), F32)] * 2
+        + [(VM, (TARGET_ROWS * LANES, LANES), F32), (VM, (40 * LANES, LANES), F32)],
+        [(edge_rows.shape, I32), (1,)],
+        "expand",
+        8,
+        flops=4 * 10**9,
+        moved=10**7,
+    )(record, table, edge_rows)
     corners = [x_low[40:], x_high[40:]]
     y_low = passed_along(jnp.concatenate([y_low] + corners, 0), "gy", -1)
     y_high = passed_along(jnp.concatenate([y_high] + corners, 0), "gy", 1)
 
+    pushed = ((32 * (tiles + 1), LANES), F32)
     (force,) = call(
         near_kernel,
-        [SM] * 3 + [VM, HBM],
+        [SM] * 3 + [VM] * 3,
         [(VM, (2 * LANES, LANES), F32)],
-        [
-            (words.shape, I32),
-            (),
-            ((TARGET_ROWS * LANES, LANES), F32),
-            ((40 * LANES, LANES), F32),
-            ((32 * (tiles + 1), LANES), F32),
-        ],
+        [pushed],
         "near",
-        flops=10**9,
-        moved=10**8,
-    )(near_tile, near_source, counts, record, words)
+        12,
+        flops=10**10,
+        moved=10**7,
+    )(near_tile, near_source, counts, targets, sources, words)
     speeds, offsets = call(
         far_kernel,
-        [SM] * 3 + [VM, HBM] + [VM] * 5,
+        [SM] * 3 + [VM] * 8,
         [(VM, (2 * LANES, LANES), F32)] * 2,
         [
-            (words.shape, I32),
-            (),
             ((2 * LANES, LANES), F32),
-            ((TARGET_ROWS * LANES, LANES), F32),
             ((40 * 40, LANES), F32),
-            ((32 * (tiles + 1), LANES), F32),
+            pushed,
         ],
         "far",
-    )(far_tile, far_source, counts, record, words, force, x_low, x_high, y_low, y_high)
+        12,
+    )(
+        far_tile, far_source, counts, record, targets, words, force,
+        x_low, x_high, y_low, y_high,
+    )
     return unpair_rows(speeds), unpair_rows(offsets)
 
 

time: 92 us -> 78.7 us (0.86)
  the two profiles are of different devices: /device:TPU:392 before, /device:TPU:231 now
where the time goes in v3:
time: 78.7 us; the launch traced here: 78.4 us
  Pallas kernels  46.7 us (59%)
  blocking collectives  16.5 us (21%)
  starting transfers between devices  14.4 us (18%)
    pallas_call x1, Pallas kernels, body(): call(near_kernel, [SM] * 3 + [VM] * 3, [(VM, (2 * LANES, LANES), F32)], [...  17.9 us
    all_to_all x1, blocking collectives, body(): lax.all_to_all(outgoing.reshape(owners, SEND_ROWS, LANES), 'gy', split_ax...  16.5 us
    ppermute x4, starting transfers between devices, passed_along(): return lax.ppermute(block, axis, route)  14.4 us
    pallas_call x1, Pallas kernels, body(): call(receive_kernel, [VM] + [HBM] * 7, [(VM, (8 * LANES, LANES), F32), (V...  9.34 us
    pallas_call x1, Pallas kernels, body(): call(send_kernel, [HBM] * 9, [(VM, (owners * SEND_ROWS, LANES), F32)] + [...  8.53 us
    pallas_call x1, Pallas kernels, body(): call(far_kernel, [SM] * 3 + [VM] * 8, [(VM, (2 * LANES, LANES), F32)] * 2...  7.28 us
    pallas_call x1, Pallas kernels, body(): call(expand_kernel, [VM, VM, HBM], [(VM, (40, LANES), F32)] * 2 + [(VM, (...  3.63 us
  transfers between devices with their start and end apart: 4, of which 0 were waited for; matrix products, arithmetic and copies ran while one was open for 0% of the time, Pallas kernels for 28%

profile of v3, /device:TPU:231, one launch (start us, length us, event | category | flops | bytes accessed | tf_op | source)
XLA Modules:
  0.0 78.4 jit_solution(8371483439952922667)
XLA Ops:
  0.6 8.5 %send.1 = (f32[768,128]{1,0:T(8,128)S(1)}, s32[388]{0:T(512)S(1)}, s32[388]{0:T(512)S(1)}, s32[388]{0:T(512)S(1)}, s32[388]{0:T(512)S(1)}, /*index=5*/s32[2]{0:T(128)S(1)}) custom-call(s32[384]{0:T(512)} %refs_0_.1, f32[256,128]{1,0:T(8,128)} %bitcast.41, f32[256,128]{1,0:T(8,128)} %bitcast.43, f32[256,128]{1,0:T(8,128)} %bitcast.45, f32[128,128]{1,0:T(8,128)} %bitcast.47, ...), custom_call_target="tpu_custom_call" | custom-call | tf_op jit(solution)/shard_map/send/pallas_call | solution.py:450
  9.2 16.5 %all_to_all.5 = f32[32,24,128]{2,1,0:T(8,128)S(1)} all-to-all(f32[32,24,128]{2,1,0:T(8,128)S(1)} %bitcast.40), channel_id=1, replica_groups=mesh['gx'=16,'gy'=32] {'gy'}, dimensions={0} | all-to-all | bytes 786432 | tf_op jit(solution)/shard_map/all_to_all | solution.py:470
  25.7 9.3 %receive.1 = (f32[1024,128]{1,0:T(8,128)S(1)}, bf16[320,768]{1,0:T(8,128)(2,1)S(1)}, f32[48,128]{1,0:T(8,128)S(1)}, f32[48,128]{1,0:T(8,128)S(1)}) custom-call(f32[768,128]{1,0:T(8,128)S(1)} %bitcast.39, f32[256,128]{1,0:T(8,128)} %bitcast.42, f32[256,128]{1,0:T(8,128)} %bitcast.44, f32[256,128]{1,0:T(8,128)} %bitcast.46, f32[128,128]{1,0:T(8,128)} %bitcast.48, ...), custom_call_target="tpu_custom_call" | custom-call | tf_op jit(solution)/shard_map/receive/pallas_call | solution.py:475
  35.0 1.9 %collective-permute-start = (f32[48,128]{1,0:T(8,128)S(1)}, f32[48,128]{1,0:T(8,128)S(1)}, u32[]{:S(2)}, u32[]{:S(2)}) collective-permute-start(f32[48,128]{1,0:T(8,128)S(1)} %get-tuple-element.28), channel_id=1, source_target_pairs={{32,0},{64,32},{96,64},{128,96},{160,128},{192,160},{224,192},{256... | collective-permute-start | bytes 73736 | tf_op jit(solution)/shard_map/ppermute | solution.py:32
  36.9 4.8 %collective-permute-start.1 = (f32[48,128]{1,0:T(8,128)S(1)}, f32[48,128]{1,0:T(8,128)S(1)}, u32[]{:S(2)}, u32[]{:S(2)}) collective-permute-start(f32[48,128]{1,0:T(8,128)S(1)} %get-tuple-element.29), channel_id=1, source_target_pairs={{0,32},{32,64},{64,96},{96,128},{128,160},{160,192},{192,224},{224... | collective-permute-start | bytes 73736 | tf_op jit(solution)/shard_map/ppermute | solution.py:32
  41.7 0.0 copy-start
  41.7 3.6 %expand.1 = (f32[40,128]{1,0:T(8,128)S(1)}, f32[40,128]{1,0:T(8,128)S(1)}, f32[9216,128]{1,0:T(8,128)S(1)}, f32[5120,128]{1,0:T(8,128)S(1)}) custom-call(f32[1024,128]{1,0:T(8,128)S(1)} %get-tuple-element.22.record, bf16[320,768]{1,0:T(8,128)(2,1)S(1)} %get-tuple-element.23.table, s32[4,1024]{1,0:T(4,128)} %rows.1), custom_call_target="tpu_custom_call" | custom-call | flops 4000000000 | bytes 10000000 | tf_op jit(solution)/shard_map/expand/pallas_call | solution.py:495
  45.4 0.0 collective-permute-done.x_low
  45.4 0.0 collective-permute-done.1.x_high
  45.4 1.9 %collective-permute-start.2 = (f32[56,128]{1,0:T(8,128)S(1)}, f32[56,128]{1,0:T(8,128)S(1)}, u32[]{:S(2)}, u32[]{:S(2)}) collective-permute-start(f32[56,128]{1,0:T(8,128)S(1)} %get-tuple-element.35), channel_id=1, source_target_pairs={{1,0},{2,1},{3,2},{4,3},{5,4},{6,5},{7,6},{8,7},{9,8},{10,9},{11,1... | collective-permute-start | bytes 86024 | tf_op jit(solution)/shard_map/ppermute | solution.py:32
  47.3 5.8 %collective-permute-start.3 = (f32[56,128]{1,0:T(8,128)S(1)}, f32[56,128]{1,0:T(8,128)S(1)}, u32[]{:S(2)}, u32[]{:S(2)}) collective-permute-start(f32[56,128]{1,0:T(8,128)S(1)} %get-tuple-element.34), channel_id=1, source_target_pairs={{0,1},{1,2},{2,3},{3,4},{4,5},{5,6},{6,7},{7,8},{8,9},{9,10},{10,1... | collective-permute-start | bytes 86024 | tf_op jit(solution)/shard_map/ppermute | solution.py:32
  53.1 0.0 copy-done
  53.1 17.9 %near.1.force = f32[256,128]{1,0:T(8,128)S(1)} custom-call(s32[388]{0:T(512)S(1)} %get-tuple-element.25.tile_ids, s32[388]{0:T(512)S(1)} %get-tuple-element.26.tile_sources, s32[2]{0:T(128)S(1)} %get-tuple-element.20.counts, f32[9216,128]{1,0:T(8,128)S(1)} %get-tuple-element.24.targets, f32[5120,128]{1,0:T(8,128)S(1)} %get-tuple-element.27.sources, ...), custom_call_target="tpu_custom_call" | custom-call | flops 10000000000 | bytes 10000000 | tf_op jit(solution)/shard_map/near/pallas_call | solution.py:511
  71.1 0.0 collective-permute-done.2.y_low
  71.1 0.0 collective-permute-done.3.y_high
  71.1 7.3 %far.1 = (f32[256,128]{1,0:T(8,128)}, f32[256,128]{1,0:T(8,128)}) custom-call(s32[388]{0:T(512)S(1)} %get-tuple-element.18.tile_ids, s32[388]{0:T(512)S(1)} %get-tuple-element.19.tile_sources, s32[2]{0:T(128)S(1)} %get-tuple-element.20.counts, f32[1024,128]{1,0:T(8,128)S(1)} %get-tuple-element.22.record, f32[9216,128]{1,0:T(8,128)S(1)} %get-tuple-element.24.targets, ...), custom_call_target="tpu_custom_call" | custom-call | tf_op jit(solution)/shard_map/far/pallas_call | solution.py:521
  (3 shorter events, 0.0 us)
Async XLA Ops:
  35.0 10.4 %collective-permute-start = (f32[48,128]{1,0:T(8,128)S(1)}, f32[48,128]{1,0:T(8,128)S(1)}, u32[]{:S(2)}, u32[]{:S(2)}) collective-permute-start(f32[48,128]{1,0:T(8,128)S(1)} %get-tuple-element.28), channel_id=1, source_target_pairs={{32,0},{64,32},{96,64},{128,96},{160,128},{192,160},{224,192},{256... | collective-permute-start | bytes 73736 | tf_op jit(solution)/shard_map/ppermute | solution.py:32
  36.9 8.4 %collective-permute-start.1 = (f32[48,128]{1,0:T(8,128)S(1)}, f32[48,128]{1,0:T(8,128)S(1)}, u32[]{:S(2)}, u32[]{:S(2)}) collective-permute-start(f32[48,128]{1,0:T(8,128)S(1)} %get-tuple-element.29), channel_id=1, source_target_pairs={{0,32},{32,64},{64,96},{96,128},{128,160},{160,192},{192,224},{224... | collective-permute-start | bytes 73736 | tf_op jit(solution)/shard_map/ppermute | solution.py:32
  41.7 11.4 %copy-start = (s32[384,2048]{1,0:T(8,128)S(1)}, s32[384,2048]{1,0:T(8,128)}, u32[]{:S(2)}) copy-start(s32[384,2048]{1,0:T(8,128)} %param.23) | copy-start | bytes 9437188
  45.4 25.7 %collective-permute-start.2 = (f32[56,128]{1,0:T(8,128)S(1)}, f32[56,128]{1,0:T(8,128)S(1)}, u32[]{:S(2)}, u32[]{:S(2)}) collective-permute-start(f32[56,128]{1,0:T(8,128)S(1)} %get-tuple-element.35), channel_id=1, source_target_pairs={{1,0},{2,1},{3,2},{4,3},{5,4},{6,5},{7,6},{8,7},{9,8},{10,9},{11,1... | collective-permute-start | bytes 86024 | tf_op jit(solution)/shard_map/ppermute | solution.py:32
  47.3 23.7 %collective-permute-start.3 = (f32[56,128]{1,0:T(8,128)S(1)}, f32[56,128]{1,0:T(8,128)S(1)}, u32[]{:S(2)}, u32[]{:S(2)}) collective-permute-start(f32[56,128]{1,0:T(8,128)S(1)} %get-tuple-element.34), channel_id=1, source_target_pairs={{0,1},{1,2},{2,3},{3,4},{4,5},{5,6},{6,7},{7,8},{8,9},{9,10},{10,1... | collective-permute-start | bytes 86024 | tf_op jit(solution)/shard_map/ppermute | solution.py:32

commit v4 on v3

--- a/solution.py
+++ b/solution.py
@@ -21,7 +21,7 @@
 MOVED_PARTS = (3, 3, 3, 3, 2, 2, 2, 2, 2)
 SEND_ROWS = 24
 SLOTS = 256
-UNROLL = 4
+UNROLL = 8
 TARGET_ROWS = 72
 MIB = 1024 * 1024
 
@@ -104,15 +104,18 @@
     held, (sem, table, coarse, spread, place, total) = refs[:9], refs[9:]
     copies = copied(zip(arguments, held), sem)
     source, pos, dis, vel, sti, den, rows, slots, news = held
-    for copy in copies:
-        copy.wait()
     for c, ref in enumerate((pos, dis)):
+        copies[1 + c].wait()
         for d in range(2):
             lookup_table(table, 2 * c + d, ref[pl.ds(d, LANES, stride=2), :])
+    copies[3].wait()
     for d in range(2):
         lookup_table(coarse, d, vel[pl.ds(d, LANES, stride=2), :])
-    lookup_table(coarse, 2, sti[...])
-    lookup_table(coarse, 3, den[...])
+    for c, ref in enumerate((sti, den)):
+        copies[4 + c].wait()
+        lookup_table(coarse, 2 + c, ref[...])
+    for copy in copies[:1] + copies[6:]:
+        copy.wait()
     total[...] = jnp.zeros_like(total)
     owners = out.shape[0] // SEND_ROWS
     tiles = source.shape[0]
@@ -320,7 +323,7 @@
             pushed[pl.ds(at + 16, 16), :] = push_y
 
 
-def gather_force(pushed, force):
+def gather_force(pushed, further, force):
     many = 64
     shape = (LANES, LANES)
     chosen = ones_where(iota(shape, 0) // 16 == iota(shape, 1) % 8)
@@ -332,9 +335,10 @@
         values = []
         for i in range(many):
             at = pl.multiple_of((group * many + i) * 32 * PER_BLOCK, 32)
-            value = pushed[pl.ds(at, 32), :]
+            value = pushed[pl.ds(at, 32), :] + further[pl.ds(at, 32), :]
             for k in range(1, PER_BLOCK):
-                value = value + pushed[pl.ds(at + 32 * k, 32), :]
+                tile = pl.ds(at + 32 * k, 32)
+                value = value + (pushed[tile, :] + further[tile, :])
             values.append(jnp.concatenate(split(value, 2), 1))
         sums = jnp.dot(jnp.concatenate(values, 0), chosen, preferred_element_type=F32)
         sums = jnp.where(own[None], sums.reshape(2 * many, 16, LANES), 0.0)
@@ -342,16 +346,15 @@
 
 
 def near_kernel(
-    tile_ids, tile_sources, counts, targets, sources, words, force, pushed
+    tile_ids, tile_sources, counts, targets, sources, words, pushed
 ):
     pushed[...] = jnp.zeros_like(pushed)
     tile_loop(counts[0], tile_ids, tile_sources, 0, words, targets, sources, pushed)
-    gather_force(pushed, force)
 
 
 def far_kernel(
-    tile_ids, tile_sources, counts, record, targets, words, force,
-    x_low, x_high, y_low, y_high, speeds, offsets, more, sources, pushed
+    tile_ids, tile_sources, counts, record, targets, words, near_pushed,
+    x_low, x_high, y_low, y_high, speeds, offsets, force, sources, pushed
 ):
     pushed[...] = jnp.zeros_like(pushed)
     halo = []
@@ -365,12 +368,12 @@
         halo.append(jnp.concatenate(edges + corners + [jnp.zeros((6, LANES), F32)], 0))
     expand_sources(halo, sources)
     tile_loop(counts[1], tile_ids, tile_sources, LANES, words, targets, sources, pushed)
-    gather_force(pushed, more)
+    gather_force(near_pushed, pushed, force)
     root = record[6 * LANES : 7 * LANES, :]
     density = record[7 * LANES : 8 * LANES, :]
     for d in range(2):
         at = pl.ds(d, LANES, stride=2)
-        total = force[at, :] + more[at, :]
+        total = force[at, :]
         speed = record[(4 + d) * LANES : (5 + d) * LANES, :] + (
             BOND_COEFFICIENT * (total * root) / density
         )
@@ -443,7 +446,7 @@
         for group in (state, moves, (edge_rows, corner_rows, tile_src))
     )
 
-    batch = 4
+    batch = 16
     listed = tiles + UNROLL
     moved_parts = first_part(9)
     held = [((2 * LANES, LANES), F32)] * 3 + [((LANES, LANES), F32)] * 2
@@ -465,7 +468,7 @@
             ((moved_parts * owners, SLOTS), F32),
         ],
         "send",
-        16,
+        24,
     )(tile_src, *state, *moves)
     got = lax.all_to_all(
         outgoing.reshape(owners, SEND_ROWS, LANES), "gy", split_axis=0, concat_axis=0, tiled=True
@@ -487,7 +490,7 @@
             ((state_parts * 64, 256), F32),
         ],
         "receive",
-        16,
+        24,
     )(got, *state, edge_rows, corner_rows)
 
     x_low = passed_along(x_low, "gx", -1)
@@ -508,13 +511,13 @@
     y_high = passed_along(jnp.concatenate([y_high] + corners, 0), "gy", 1)
 
     pushed = ((32 * (tiles + 1), LANES), F32)
-    (force,) = call(
+    (near_pushed,) = call(
         near_kernel,
         [SM] * 3 + [VM] * 3,
-        [(VM, (2 * LANES, LANES), F32)],
-        [pushed],
+        [(VM, *pushed)],
+        [],
         "near",
-        12,
+        8,
         flops=10**10,
         moved=10**7,
     )(near_tile, near_source, counts, targets, sources, words)
@@ -530,7 +533,7 @@
         "far",
         12,
     )(
-        far_tile, far_source, counts, record, targets, words, force,
+        far_tile, far_source, counts, record, targets, words, near_pushed,
         x_low, x_high, y_low, y_high,
     )
     return unpair_rows(speeds), unpair_rows(offsets)

time: 78.7 us -> 76.3 us (0.970)
  Pallas kernels: 46.7 us -> 44.2 us
    pallas_call x1, Pallas kernels: 9.34 us -> 8.05 us  [body(): call(receive_kernel, [VM] + [HBM] * 7, [(VM, (8 * LANES, LANES), F32), (V...]
    pallas_call x1, Pallas kernels: 17.9 us -> 16.8 us  [body(): call(near_kernel, [SM] * 3 + [VM] * 3, [(VM, *pushed)], [], 'near', 8, fl...]
  transfers between devices with their start and end apart: 4 -> 4, of which waited for: 0 -> 0; matrix products, arithmetic and copies ran while one was open for 0% -> 0% of each run, Pallas kernels for 28% -> 27%
where the time goes in v4:
time: 76.3 us; the launch traced here: 76.1 us
  Pallas kernels  44.2 us (58%)
  blocking collectives  16.5 us (22%)
  starting transfers between devices  14.5 us (19%)
    pallas_call x1, Pallas kernels, body(): call(near_kernel, [SM] * 3 + [VM] * 3, [(VM, *pushed)], [], 'near', 8, fl...  16.8 us
    all_to_all x1, blocking collectives, body(): lax.all_to_all(outgoing.reshape(owners, SEND_ROWS, LANES), 'gy', split_ax...  16.5 us
    ppermute x4, starting transfers between devices, passed_along(): return lax.ppermute(block, axis, route)  14.5 us
    pallas_call x1, Pallas kernels, body(): call(send_kernel, [HBM] * 9, [(VM, (owners * SEND_ROWS, LANES), F32)] + [...  8.18 us
    pallas_call x1, Pallas kernels, body(): call(receive_kernel, [VM] + [HBM] * 7, [(VM, (8 * LANES, LANES), F32), (V...  8.05 us
    pallas_call x1, Pallas kernels, body(): call(far_kernel, [SM] * 3 + [VM] * 8, [(VM, (2 * LANES, LANES), F32)] * 2...  7.53 us
    pallas_call x1, Pallas kernels, body(): call(expand_kernel, [VM, VM, HBM], [(VM, (40, LANES), F32)] * 2 + [(VM, (...  3.65 us
  transfers between devices with their start and end apart: 4, of which 0 were waited for; matrix products, arithmetic and copies ran while one was open for 0% of the time, Pallas kernels for 27%

profile of v4, /device:TPU:231, one launch (start us, length us, event | category | flops | bytes accessed | tf_op | source)
XLA Modules:
  0.0 76.1 jit_solution(17315833415374658402)
XLA Ops:
  0.6 8.2 %send.1 = (f32[768,128]{1,0:T(8,128)S(1)}, s32[392]{0:T(512)S(1)}, s32[392]{0:T(512)S(1)}, s32[392]{0:T(512)S(1)}, s32[392]{0:T(512)S(1)}, /*index=5*/s32[2]{0:T(128)S(1)}) custom-call(s32[384]{0:T(512)} %refs_0_.1, f32[256,128]{1,0:T(8,128)} %bitcast.41, f32[256,128]{1,0:T(8,128)} %bitcast.43, f32[256,128]{1,0:T(8,128)} %bitcast.45, f32[128,128]{1,0:T(8,128)} %bitcast.47, ...), custom_call_target="tpu_custom_call" | custom-call | tf_op jit(solution)/shard_map/send/pallas_call | solution.py:453
  8.8 16.5 %all_to_all.5 = f32[32,24,128]{2,1,0:T(8,128)S(1)} all-to-all(f32[32,24,128]{2,1,0:T(8,128)S(1)} %bitcast.40), channel_id=1, replica_groups=mesh['gx'=16,'gy'=32] {'gy'}, dimensions={0} | all-to-all | bytes 786432 | tf_op jit(solution)/shard_map/all_to_all | solution.py:473
  25.3 8.1 %receive.1 = (f32[1024,128]{1,0:T(8,128)S(1)}, bf16[320,768]{1,0:T(8,128)(2,1)S(1)}, f32[48,128]{1,0:T(8,128)S(1)}, f32[48,128]{1,0:T(8,128)S(1)}) custom-call(f32[768,128]{1,0:T(8,128)S(1)} %bitcast.39, f32[256,128]{1,0:T(8,128)} %bitcast.42, f32[256,128]{1,0:T(8,128)} %bitcast.44, f32[256,128]{1,0:T(8,128)} %bitcast.46, f32[128,128]{1,0:T(8,128)} %bitcast.48, ...), custom_call_target="tpu_custom_call" | custom-call | tf_op jit(solution)/shard_map/receive/pallas_call | solution.py:478
  33.4 1.9 %collective-permute-start = (f32[48,128]{1,0:T(8,128)S(1)}, f32[48,128]{1,0:T(8,128)S(1)}, u32[]{:S(2)}, u32[]{:S(2)}) collective-permute-start(f32[48,128]{1,0:T(8,128)S(1)} %get-tuple-element.28), channel_id=1, source_target_pairs={{32,0},{64,32},{96,64},{128,96},{160,128},{192,160},{224,192},{256... | collective-permute-start | bytes 73736 | tf_op jit(solution)/shard_map/ppermute | solution.py:32
  35.3 5.0 %collective-permute-start.1 = (f32[48,128]{1,0:T(8,128)S(1)}, f32[48,128]{1,0:T(8,128)S(1)}, u32[]{:S(2)}, u32[]{:S(2)}) collective-permute-start(f32[48,128]{1,0:T(8,128)S(1)} %get-tuple-element.29), channel_id=1, source_target_pairs={{0,32},{32,64},{64,96},{96,128},{128,160},{160,192},{192,224},{224... | collective-permute-start | bytes 73736 | tf_op jit(solution)/shard_map/ppermute | solution.py:32
  40.3 0.0 copy-start
  40.3 3.6 %expand.1 = (f32[40,128]{1,0:T(8,128)S(1)}, f32[40,128]{1,0:T(8,128)S(1)}, f32[9216,128]{1,0:T(8,128)S(1)}, f32[5120,128]{1,0:T(8,128)S(1)}) custom-call(f32[1024,128]{1,0:T(8,128)S(1)} %get-tuple-element.22.record, bf16[320,768]{1,0:T(8,128)(2,1)S(1)} %get-tuple-element.23.table, s32[4,1024]{1,0:T(4,128)} %rows.1), custom_call_target="tpu_custom_call" | custom-call | flops 4000000000 | bytes 10000000 | tf_op jit(solution)/shard_map/expand/pallas_call | solution.py:498
  43.9 0.0 collective-permute-done.1.x_high
  43.9 0.0 collective-permute-done.x_low
  44.0 1.9 %collective-permute-start.2 = (f32[56,128]{1,0:T(8,128)S(1)}, f32[56,128]{1,0:T(8,128)S(1)}, u32[]{:S(2)}, u32[]{:S(2)}) collective-permute-start(f32[56,128]{1,0:T(8,128)S(1)} %get-tuple-element.35), channel_id=1, source_target_pairs={{1,0},{2,1},{3,2},{4,3},{5,4},{6,5},{7,6},{8,7},{9,8},{10,9},{11,1... | collective-permute-start | bytes 86024 | tf_op jit(solution)/shard_map/ppermute | solution.py:32
  45.9 5.8 %collective-permute-start.3 = (f32[56,128]{1,0:T(8,128)S(1)}, f32[56,128]{1,0:T(8,128)S(1)}, u32[]{:S(2)}, u32[]{:S(2)}) collective-permute-start(f32[56,128]{1,0:T(8,128)S(1)} %get-tuple-element.34), channel_id=1, source_target_pairs={{0,1},{1,2},{2,3},{3,4},{4,5},{5,6},{6,7},{7,8},{8,9},{9,10},{10,1... | collective-permute-start | bytes 86024 | tf_op jit(solution)/shard_map/ppermute | solution.py:32
  51.7 0.0 copy-done
  51.7 16.8 %near.1.near_pushed = f32[12320,128]{1,0:T(8,128)S(1)} custom-call(s32[392]{0:T(512)S(1)} %get-tuple-element.25.tile_ids, s32[392]{0:T(512)S(1)} %get-tuple-element.26.tile_sources, s32[2]{0:T(128)S(1)} %get-tuple-element.20.counts, f32[9216,128]{1,0:T(8,128)S(1)} %get-tuple-element.24.targets, f32[5120,128]{1,0:T(8,128)S(1)} %get-tuple-element.27.sources, ...), custom_call_target="tpu_custom_call" | custom-call | flops 10000000000 | bytes 10000000 | tf_op jit(solution)/shard_map/near/pallas_call | solution.py:514
  68.5 0.0 collective-permute-done.2.y_low
  68.5 0.0 collective-permute-done.3.y_high
  68.5 7.5 %far.1 = (f32[256,128]{1,0:T(8,128)}, f32[256,128]{1,0:T(8,128)}) custom-call(s32[392]{0:T(512)S(1)} %get-tuple-element.18.tile_ids, s32[392]{0:T(512)S(1)} %get-tuple-element.19.tile_sources, s32[2]{0:T(128)S(1)} %get-tuple-element.20.counts, f32[1024,128]{1,0:T(8,128)S(1)} %get-tuple-element.22.record, f32[9216,128]{1,0:T(8,128)S(1)} %get-tuple-element.24.targets, ...), custom_call_target="tpu_custom_call" | custom-call | tf_op jit(solution)/shard_map/far/pallas_call | solution.py:524
  (3 shorter events, 0.0 us)
Async XLA Ops:
  33.4 10.6 %collective-permute-start = (f32[48,128]{1,0:T(8,128)S(1)}, f32[48,128]{1,0:T(8,128)S(1)}, u32[]{:S(2)}, u32[]{:S(2)}) collective-permute-start(f32[48,128]{1,0:T(8,128)S(1)} %get-tuple-element.28), channel_id=1, source_target_pairs={{32,0},{64,32},{96,64},{128,96},{160,128},{192,160},{224,192},{256... | collective-permute-start | bytes 73736 | tf_op jit(solution)/shard_map/ppermute | solution.py:32
  35.3 8.6 %collective-permute-start.1 = (f32[48,128]{1,0:T(8,128)S(1)}, f32[48,128]{1,0:T(8,128)S(1)}, u32[]{:S(2)}, u32[]{:S(2)}) collective-permute-start(f32[48,128]{1,0:T(8,128)S(1)} %get-tuple-element.29), channel_id=1, source_target_pairs={{0,32},{32,64},{64,96},{96,128},{128,160},{160,192},{192,224},{224... | collective-permute-start | bytes 73736 | tf_op jit(solution)/shard_map/ppermute | solution.py:32
  40.3 11.4 %copy-start = (s32[384,2048]{1,0:T(8,128)S(1)}, s32[384,2048]{1,0:T(8,128)}, u32[]{:S(2)}) copy-start(s32[384,2048]{1,0:T(8,128)} %param.23) | copy-start | bytes 9437188
  44.0 24.5 %collective-permute-start.2 = (f32[56,128]{1,0:T(8,128)S(1)}, f32[56,128]{1,0:T(8,128)S(1)}, u32[]{:S(2)}, u32[]{:S(2)}) collective-permute-start(f32[56,128]{1,0:T(8,128)S(1)} %get-tuple-element.35), channel_id=1, source_target_pairs={{1,0},{2,1},{3,2},{4,3},{5,4},{6,5},{7,6},{8,7},{9,8},{10,9},{11,1... | collective-permute-start | bytes 86024 | tf_op jit(solution)/shard_map/ppermute | solution.py:32
  45.9 22.6 %collective-permute-start.3 = (f32[56,128]{1,0:T(8,128)S(1)}, f32[56,128]{1,0:T(8,128)S(1)}, u32[]{:S(2)}, u32[]{:S(2)}) collective-permute-start(f32[56,128]{1,0:T(8,128)S(1)} %get-tuple-element.34), channel_id=1, source_target_pairs={{0,1},{1,2},{2,3},{3,4},{4,5},{5,6},{6,7},{7,8},{8,9},{9,10},{10,1... | collective-permute-start | bytes 86024 | tf_op jit(solution)/shard_map/ppermute | solution.py:32

commit v5 on v4

--- a/solution.py
+++ b/solution.py
@@ -224,17 +224,13 @@
 
 
 def look_up_edges(table, edge_rows, bundles):
-    half = edge_rows.shape[1] // 512
-
-    @pl.loop(0, half)
-    def _(q):
-        for edge, bundle in bundles:
-            for i in range(2):
-                at = q + i * half
-                index = edge_rows[edge : edge + 1, pl.ds(pl.multiple_of(at * 256, 256), 256)]
-                for c, value in enumerate(looked_up((table,), index)):
-                    bundle[pl.ds(c * 8 + 2 * at, 1), :] = value[:, :LANES]
-                    bundle[pl.ds(c * 8 + 2 * at + 1, 1), :] = value[:, LANES:]
+    for edge, bundle in bundles:
+        for at in range(edge_rows.shape[1] // 256):
+            index = edge_rows[edge : edge + 1, at * 256 : (at + 1) * 256]
+            for c, value in enumerate(looked_up((table,), index)):
+                row = c * 8 + 2 * at
+                bundle[row : row + 1, :] = value[:, :LANES]
+                bundle[row + 1 : row + 2, :] = value[:, LANES:]
 
 
 def expand_kernel(record, table, rows, y_low, y_high, targets, sources, edge_rows, sem):

time: 76.3 us -> 75.6 us (level)
  the two profiles are of different devices: /device:TPU:231 before, /device:TPU:103 now
where the time goes in v5:
time: 75.6 us; the launch traced here: 75.4 us
  Pallas kernels  43.5 us (58%)
  blocking collectives  16.5 us (22%)
  starting transfers between devices  14.5 us (19%)
  between operations  0.76 us (1%)
    pallas_call x1, Pallas kernels, body(): call(near_kernel, [SM] * 3 + [VM] * 3, [(VM, *pushed)], [], 'near', 8, fl...  17.3 us
    all_to_all x1, blocking collectives, body(): lax.all_to_all(outgoing.reshape(owners, SEND_ROWS, LANES), 'gy', split_ax...  16.5 us
    ppermute x4, starting transfers between devices, passed_along(): return lax.ppermute(block, axis, route)  14.5 us
    pallas_call x1, Pallas kernels, body(): call(send_kernel, [HBM] * 9, [(VM, (owners * SEND_ROWS, LANES), F32)] + [...  8.17 us
    pallas_call x1, Pallas kernels, body(): call(receive_kernel, [VM] + [HBM] * 7, [(VM, (8 * LANES, LANES), F32), (V...  7.52 us
    pallas_call x1, Pallas kernels, body(): call(far_kernel, [SM] * 3 + [VM] * 8, [(VM, (2 * LANES, LANES), F32)] * 2...  7.11 us
    pallas_call x1, Pallas kernels, body(): call(expand_kernel, [VM, VM, HBM], [(VM, (40, LANES), F32)] * 2 + [(VM, (...  3.46 us
  transfers between devices with their start and end apart: 4, of which 0 were waited for; matrix products, arithmetic and copies ran while one was open for 0% of the time, Pallas kernels for 27%

profile of v5, /device:TPU:103, one launch (start us, length us, event | category | flops | bytes accessed | tf_op | source)
XLA Modules:
  0.0 75.4 jit_solution(9623116674348059840)
XLA Ops:
  0.6 8.2 %send.1 = (f32[768,128]{1,0:T(8,128)S(1)}, s32[392]{0:T(512)S(1)}, s32[392]{0:T(512)S(1)}, s32[392]{0:T(512)S(1)}, s32[392]{0:T(512)S(1)}, /*index=5*/s32[2]{0:T(128)S(1)}) custom-call(s32[384]{0:T(512)} %refs_0_.1, f32[256,128]{1,0:T(8,128)} %bitcast.41, f32[256,128]{1,0:T(8,128)} %bitcast.43, f32[256,128]{1,0:T(8,128)} %bitcast.45, f32[128,128]{1,0:T(8,128)} %bitcast.47, ...), custom_call_target="tpu_custom_call" | custom-call | tf_op jit(solution)/shard_map/send/pallas_call | solution.py:449
  8.8 16.5 %all_to_all.5 = f32[32,24,128]{2,1,0:T(8,128)S(1)} all-to-all(f32[32,24,128]{2,1,0:T(8,128)S(1)} %bitcast.40), channel_id=1, replica_groups=mesh['gx'=16,'gy'=32] {'gy'}, dimensions={0} | all-to-all | bytes 786432 | tf_op jit(solution)/shard_map/all_to_all | solution.py:469
  25.3 7.5 %receive.1 = (f32[1024,128]{1,0:T(8,128)S(1)}, bf16[320,768]{1,0:T(8,128)(2,1)S(1)}, f32[48,128]{1,0:T(8,128)S(1)}, f32[48,128]{1,0:T(8,128)S(1)}) custom-call(f32[768,128]{1,0:T(8,128)S(1)} %bitcast.39, f32[256,128]{1,0:T(8,128)} %bitcast.42, f32[256,128]{1,0:T(8,128)} %bitcast.44, f32[256,128]{1,0:T(8,128)} %bitcast.46, f32[128,128]{1,0:T(8,128)} %bitcast.48, ...), custom_call_target="tpu_custom_call" | custom-call | tf_op jit(solution)/shard_map/receive/pallas_call | solution.py:474
  32.8 1.9 %collective-permute-start = (f32[48,128]{1,0:T(8,128)S(1)}, f32[48,128]{1,0:T(8,128)S(1)}, u32[]{:S(2)}, u32[]{:S(2)}) collective-permute-start(f32[48,128]{1,0:T(8,128)S(1)} %get-tuple-element.28), channel_id=1, source_target_pairs={{32,0},{64,32},{96,64},{128,96},{160,128},{192,160},{224,192},{256... | collective-permute-start | bytes 73736 | tf_op jit(solution)/shard_map/ppermute | solution.py:32
  34.8 4.9 %collective-permute-start.1 = (f32[48,128]{1,0:T(8,128)S(1)}, f32[48,128]{1,0:T(8,128)S(1)}, u32[]{:S(2)}, u32[]{:S(2)}) collective-permute-start(f32[48,128]{1,0:T(8,128)S(1)} %get-tuple-element.29), channel_id=1, source_target_pairs={{0,32},{32,64},{64,96},{96,128},{128,160},{160,192},{192,224},{224... | collective-permute-start | bytes 73736 | tf_op jit(solution)/shard_map/ppermute | solution.py:32
  39.7 0.0 copy-start
  39.7 3.5 %expand.1 = (f32[40,128]{1,0:T(8,128)S(1)}, f32[40,128]{1,0:T(8,128)S(1)}, f32[9216,128]{1,0:T(8,128)S(1)}, f32[5120,128]{1,0:T(8,128)S(1)}) custom-call(f32[1024,128]{1,0:T(8,128)S(1)} %get-tuple-element.22.record, bf16[320,768]{1,0:T(8,128)(2,1)S(1)} %get-tuple-element.23.table, s32[4,1024]{1,0:T(4,128)} %rows.1), custom_call_target="tpu_custom_call" | custom-call | flops 4000000000 | bytes 10000000 | tf_op jit(solution)/shard_map/expand/pallas_call | solution.py:494
  43.2 0.0 collective-permute-done.1.x_high
  43.2 0.0 collective-permute-done.x_low
  43.2 1.9 %collective-permute-start.2 = (f32[56,128]{1,0:T(8,128)S(1)}, f32[56,128]{1,0:T(8,128)S(1)}, u32[]{:S(2)}, u32[]{:S(2)}) collective-permute-start(f32[56,128]{1,0:T(8,128)S(1)} %get-tuple-element.35), channel_id=1, source_target_pairs={{1,0},{2,1},{3,2},{4,3},{5,4},{6,5},{7,6},{8,7},{9,8},{10,9},{11,1... | collective-permute-start | bytes 86024 | tf_op jit(solution)/shard_map/ppermute | solution.py:32
  45.2 5.8 %collective-permute-start.3 = (f32[56,128]{1,0:T(8,128)S(1)}, f32[56,128]{1,0:T(8,128)S(1)}, u32[]{:S(2)}, u32[]{:S(2)}) collective-permute-start(f32[56,128]{1,0:T(8,128)S(1)} %get-tuple-element.34), channel_id=1, source_target_pairs={{0,1},{1,2},{2,3},{3,4},{4,5},{5,6},{6,7},{7,8},{8,9},{9,10},{10,1... | collective-permute-start | bytes 86024 | tf_op jit(solution)/shard_map/ppermute | solution.py:32
  50.9 0.0 copy-done
  50.9 17.3 %near.1.near_pushed = f32[12320,128]{1,0:T(8,128)S(1)} custom-call(s32[392]{0:T(512)S(1)} %get-tuple-element.25.tile_ids, s32[392]{0:T(512)S(1)} %get-tuple-element.26.tile_sources, s32[2]{0:T(128)S(1)} %get-tuple-element.20.counts, f32[9216,128]{1,0:T(8,128)S(1)} %get-tuple-element.24.targets, f32[5120,128]{1,0:T(8,128)S(1)} %get-tuple-element.27.sources, ...), custom_call_target="tpu_custom_call" | custom-call | flops 10000000000 | bytes 10000000 | tf_op jit(solution)/shard_map/near/pallas_call | solution.py:510
  68.2 0.0 collective-permute-done.2.y_low
  68.2 0.0 collective-permute-done.3.y_high
  68.2 7.1 %far.1 = (f32[256,128]{1,0:T(8,128)}, f32[256,128]{1,0:T(8,128)}) custom-call(s32[392]{0:T(512)S(1)} %get-tuple-element.18.tile_ids, s32[392]{0:T(512)S(1)} %get-tuple-element.19.tile_sources, s32[2]{0:T(128)S(1)} %get-tuple-element.20.counts, f32[1024,128]{1,0:T(8,128)S(1)} %get-tuple-element.22.record, f32[9216,128]{1,0:T(8,128)S(1)} %get-tuple-element.24.targets, ...), custom_call_target="tpu_custom_call" | custom-call | tf_op jit(solution)/shard_map/far/pallas_call | solution.py:520
  (3 shorter events, 0.0 us)
Async XLA Ops:
  32.8 10.4 %collective-permute-start = (f32[48,128]{1,0:T(8,128)S(1)}, f32[48,128]{1,0:T(8,128)S(1)}, u32[]{:S(2)}, u32[]{:S(2)}) collective-permute-start(f32[48,128]{1,0:T(8,128)S(1)} %get-tuple-element.28), channel_id=1, source_target_pairs={{32,0},{64,32},{96,64},{128,96},{160,128},{192,160},{224,192},{256... | collective-permute-start | bytes 73736 | tf_op jit(solution)/shard_map/ppermute | solution.py:32
  34.8 8.4 %collective-permute-start.1 = (f32[48,128]{1,0:T(8,128)S(1)}, f32[48,128]{1,0:T(8,128)S(1)}, u32[]{:S(2)}, u32[]{:S(2)}) collective-permute-start(f32[48,128]{1,0:T(8,128)S(1)} %get-tuple-element.29), channel_id=1, source_target_pairs={{0,32},{32,64},{64,96},{96,128},{128,160},{160,192},{192,224},{224... | collective-permute-start | bytes 73736 | tf_op jit(solution)/shard_map/ppermute | solution.py:32
  39.7 11.2 %copy-start = (s32[384,2048]{1,0:T(8,128)S(1)}, s32[384,2048]{1,0:T(8,128)}, u32[]{:S(2)}) copy-start(s32[384,2048]{1,0:T(8,128)} %param.23) | copy-start | bytes 9437188
  43.2 25.0 %collective-permute-start.2 = (f32[56,128]{1,0:T(8,128)S(1)}, f32[56,128]{1,0:T(8,128)S(1)}, u32[]{:S(2)}, u32[]{:S(2)}) collective-permute-start(f32[56,128]{1,0:T(8,128)S(1)} %get-tuple-element.35), channel_id=1, source_target_pairs={{1,0},{2,1},{3,2},{4,3},{5,4},{6,5},{7,6},{8,7},{9,8},{10,9},{11,1... | collective-permute-start | bytes 86024 | tf_op jit(solution)/shard_map/ppermute | solution.py:32
  45.2 23.1 %collective-permute-start.3 = (f32[56,128]{1,0:T(8,128)S(1)}, f32[56,128]{1,0:T(8,128)S(1)}, u32[]{:S(2)}, u32[]{:S(2)}) collective-permute-start(f32[56,128]{1,0:T(8,128)S(1)} %get-tuple-element.34), channel_id=1, source_target_pairs={{0,1},{1,2},{2,3},{3,4},{4,5},{5,6},{6,7},{7,8},{8,9},{9,10},{10,1... | collective-permute-start | bytes 86024 | tf_op jit(solution)/shard_map/ppermute | solution.py:32
